TPU v7x, 256 devices: a whole 4x4x8 slice. The times are simulated.
256 devices in a mesh: seq: 64 (over z, x_lo, y), head: 4 (over x_hi, core).
Axes of the slice: x: 4 (x_hi: 2, x_lo: 2; x = x_hi * 2 + x_lo), y: 4, z: 8, core: 2. Of those that a mesh axis runs over, the one named last changes fastest.
Arguments:
- tokens: bfloat16 [65536, 2048], P('seq', 'head'), may hold values from -20 to 20
- w_query: bfloat16 [2048, 2048], P(None, 'head'), may hold values from -1 to 1
- w_key: bfloat16 [2048, 2048], P(None, 'head'), may hold values from -1 to 1
- w_value: bfloat16 [2048, 2048], P(None, 'head'), may hold values from -0.125 to 0.125
- w_out: bfloat16 [2048, 2048], P('head'), may hold values from -0.125 to 0.125
Outputs:
- attended: bfloat16 [65536, 2048], P(('seq', 'head'))
All inputs are finite; a program needn't handle non-finite values.
Results may differ from a plain program's by a relative error of at most 0.04.
Values may be sent and summed in bfloat16 or wider, within the bound.
A program may use at most 128 MiB of HBM per device.

v0:
```python
import jax
import jax.numpy as jnp
from jax import lax
from jax.sharding import PartitionSpec as P

DH = 128
STRIDE = 256


def from_behind(value, axis, by):
    peers = lax.axis_size(axis)
    pairs = [(i, i + by) for i in range(peers) if 0 <= i + by < peers]
    return lax.ppermute(value, axis, pairs)


def shards(tokens, w_query, w_key, w_value, w_out):
    tok_rows = tokens.shape[0]
    head_width = w_query.shape[1]
    head_count = head_width // DH
    score_scale = DH ** (-0.5)
    shard_piece = lax.all_gather(tokens, "head", axis=1, tiled=True)
    query_full, key_full, value_full = tuple(
        (
            jnp.dot(shard_piece, weight, preferred_element_type=jnp.float32)
            for weight in (w_query, w_key, w_value)
        )
    )
    query = query_full.astype(jnp.bfloat16).reshape(tok_rows, head_count, DH)
    key_heads = key_full.astype(jnp.bfloat16).reshape(tok_rows, head_count, DH)
    value_heads = value_full.astype(jnp.bfloat16).reshape(tok_rows, head_count, DH)
    prev_keys, prev_values = from_behind((key_heads[-STRIDE:], value_heads[-STRIDE:]), "seq", 1)
    blocks = tok_rows // STRIDE
    extended_keys = jnp.concatenate([prev_keys, key_heads], 0)
    extended_values = jnp.concatenate([prev_values, value_heads], 0)
    window_keys = jnp.concatenate(
        [
            extended_keys[:tok_rows].reshape(blocks, STRIDE, head_count, DH),
            extended_keys[STRIDE:].reshape(blocks, STRIDE, head_count, DH),
        ],
        1,
    )
    window_values = jnp.concatenate(
        [
            extended_values[:tok_rows].reshape(blocks, STRIDE, head_count, DH),
            extended_values[STRIDE:].reshape(blocks, STRIDE, head_count, DH),
        ],
        1,
    )
    query_blocks = query.reshape(blocks, STRIDE, head_count, DH)
    scores = (
        jnp.einsum("bthd,buhd->bhtu", query_blocks, window_keys, preferred_element_type=jnp.float32)
        * score_scale
    )
    first_position = lax.axis_index("seq") * tok_rows
    block_index = jnp.arange(blocks)[:, None, None, None]
    query_index = jnp.arange(STRIDE)[None, None, :, None]
    key_index = jnp.arange(2 * STRIDE)[None, None, None, :]
    allowed = (
        (key_index > query_index)
        & (key_index <= query_index + STRIDE)
        & (first_position + block_index * STRIDE + key_index - STRIDE >= 0)
    )
    local_top = jnp.max(jnp.where(allowed, scores, -1e30), axis=-1)
    local_weights = jnp.where(allowed, jnp.exp(scores - local_top[..., None]), 0.0)
    local_total = jnp.sum(local_weights, axis=-1)
    local_out = jnp.einsum(
        "bhtu,buhd->bthd",
        local_weights.astype(jnp.bfloat16),
        window_values,
        preferred_element_type=jnp.float32,
    )
    local_out = local_out.reshape(tok_rows, head_count, DH)
    local_top = local_top.transpose(0, 2, 1).reshape(tok_rows, head_count)
    local_total = local_total.transpose(0, 2, 1).reshape(tok_rows, head_count)
    row_count = tok_rows // STRIDE
    query_class = lax.all_to_all(
        query.reshape(row_count, STRIDE, head_count, DH),
        "seq",
        split_axis=1,
        concat_axis=0,
        tiled=True,
    )
    key_class = lax.all_to_all(
        key_heads.reshape(row_count, STRIDE, head_count, DH),
        "seq",
        split_axis=1,
        concat_axis=0,
        tiled=True,
    )
    value_class = lax.all_to_all(
        value_heads.reshape(row_count, STRIDE, head_count, DH),
        "seq",
        split_axis=1,
        concat_axis=0,
        tiled=True,
    )
    row_total = query_class.shape[0]
    class_scores = (
        jnp.einsum("rchd,schd->chrs", query_class, key_class, preferred_element_type=jnp.float32)
        * score_scale
    )
    earlier = (
        jnp.arange(row_total)[None, None, :, None] > jnp.arange(row_total)[None, None, None, :]
    )
    class_top = jnp.max(jnp.where(earlier, class_scores, -1e30), axis=-1)
    class_weights = jnp.where(earlier, jnp.exp(class_scores - class_top[..., None]), 0.0)
    class_total = jnp.sum(class_weights, axis=-1)
    summed = jnp.einsum(
        "chrs,schd->rchd",
        class_weights.astype(jnp.bfloat16),
        value_class,
        preferred_element_type=jnp.float32,
    )
    floor_total = jnp.maximum(class_total, 1.0).transpose(2, 0, 1)
    class_out = (summed / floor_total[..., None]).astype(jnp.bfloat16)
    class_top_rows = class_top.transpose(2, 0, 1)
    class_total_rows = class_total.transpose(2, 0, 1)
    column_out = class_out
    column_top = class_top_rows
    column_total = class_total_rows
    column_out, column_top, column_total = (
        lax.all_to_all(column_out, "seq", split_axis=0, concat_axis=1, tiled=True),
        lax.all_to_all(
            column_top.astype(jnp.bfloat16), "seq", split_axis=0, concat_axis=1, tiled=True
        ).astype(column_top.dtype),
        lax.all_to_all(
            column_total.astype(jnp.bfloat16), "seq", split_axis=0, concat_axis=1, tiled=True
        ).astype(column_total.dtype),
    )
    column_out = column_out.reshape(tok_rows, head_count, DH)
    column_top = column_top.reshape(tok_rows, head_count)
    column_total = column_total.reshape(tok_rows, head_count)
    top_score = jnp.maximum(local_top, column_top)
    local_weight = jnp.exp(local_top - top_score)
    column_weight = column_total * jnp.exp(column_top - top_score)
    denominator = local_total * local_weight + column_weight
    mixed = (
        local_out * local_weight[..., None]
        + column_out.astype(jnp.float32) * column_weight[..., None]
    ) / denominator[..., None]
    mixed = mixed.astype(jnp.bfloat16).reshape(tok_rows, head_width)
    return lax.psum_scatter(
        jnp.dot(mixed, w_out, preferred_element_type=jnp.float32).astype(jnp.bfloat16),
        "head",
        scatter_dimension=0,
        tiled=True,
    )


def solution(mesh):
    in_specs = (
        P("seq", "head"),
        P(None, "head"),
        P(None, "head"),
        P(None, "head"),
        P("head", None),
    )
    out_specs = P(("seq", "head"), None)
    return jax.shard_map(shards, mesh=mesh, in_specs=in_specs, out_specs=out_specs, check_vma=False)
```

profile of v0, /device:TPU:1, one launch (start us, length us, event | category | flops | bytes accessed | tf_op | source)
XLA Modules:
  0.0 343.3 jit_solution(17285253116269827363)
XLA Ops:
  7.3 47.2 %all-gather.2.cloned.1.call-done = bf16[1024,2048]{1,0:T(8,128)(2,1)} async-done(((bf16[1024,512]{1,0:T(8,128)(2,1)}), bf16[1024,2048]{1,0:T(8,128)(2,1)}) %all-gather.2.cloned.1.call-update) | async-done | bytes 4194320 | tf_op jit(solution)/shard_map/all_gather | solution.py:21
  54.5 6.2 %convolution_convert_fusion.1 = bf16[1024,512]{0,1:T(8,128)(2,1)} fusion(bf16[1024,2048]{1,0:T(8,128)(2,1)} %all-gather.2.cloned.1.call-done, bf16[2048,512]{1,0:T(8,128)(2,1)} %param.7), kind=kOutput, calls=%fused_computation.35 | convolution fusion | flops 2148007936 | bytes 7340032 | tf_op jit(solution)/shard_map/dot_general | solution.py:24
  64.8 10.5 %all-to-all-start.1 = ((bf16[4,256,4,128]{3,2,0,1:T(4,128)(2,1)}), bf16[4,256,4,128]{3,2,0,1:T(4,128)(2,1)}, u32[]{:S(2)}, u32[]{:S(2)}) async-start(bf16[4,256,4,128]{3,2,0,1:T(4,128)(2,1)} %copy.113), calls=%async_computation.1 | async-start | bytes 2097152 | tf_op jit(solution)/shard_map/all_to_all | solution.py:83
  75.2 6.2 %convolution_convert_fusion.2 = bf16[1024,512]{1,0:T(8,128)(2,1)} fusion(bf16[1024,2048]{1,0:T(8,128)(2,1)} %all-gather.2.cloned.1.call-done, bf16[2048,512]{1,0:T(8,128)(2,1)} %param.6), kind=kOutput, calls=%fused_computation.36 | convolution fusion | flops 2148007936 | bytes 7340032 | tf_op jit(solution)/shard_map/dot_general | solution.py:24
  86.1 15.6 %all-to-all-done.1 = bf16[4,256,4,128]{3,2,0,1:T(4,128)(2,1)} async-done(((bf16[4,256,4,128]{3,2,0,1:T(4,128)(2,1)}), bf16[4,256,4,128]{3,2,0,1:T(4,128)(2,1)}, u32[]{:S(2)}, u32[]{:S(2)}) %all-to-all-start.1) | async-done | bytes 1048608 | tf_op jit(solution)/shard_map/all_to_all | solution.py:83
  101.8 7.7 %all-to-all-start = ((bf16[4,256,4,128]{3,2,0,1:T(4,128)(2,1)}), bf16[4,256,4,128]{3,2,0,1:T(4,128)(2,1)}, u32[]{:S(2)}, u32[]{:S(2)}) async-start(bf16[4,256,4,128]{3,2,0,1:T(4,128)(2,1)} %copy.111), calls=%async_computation | async-start | bytes 2097152 | tf_op jit(solution)/shard_map/all_to_all | solution.py:76
  109.4 6.2 %convolution_convert_fusion.3 = bf16[1024,512]{0,1:T(8,128)(2,1)} fusion(bf16[1024,2048]{1,0:T(8,128)(2,1)} %all-gather.2.cloned.1.call-done, bf16[2048,512]{1,0:T(8,128)(2,1)} %param.8), kind=kOutput, calls=%fused_computation.37 | convolution fusion | flops 2148007936 | bytes 7340032 | tf_op jit(solution)/shard_map/dot_general | solution.py:24
  121.2 13.1 %all-to-all-done = bf16[4,256,4,128]{3,2,0,1:T(4,128)(2,1)} async-done(((bf16[4,256,4,128]{3,2,0,1:T(4,128)(2,1)}), bf16[4,256,4,128]{3,2,0,1:T(4,128)(2,1)}, u32[]{:S(2)}, u32[]{:S(2)}) %all-to-all-start) | async-done | bytes 1048608 | tf_op jit(solution)/shard_map/all_to_all | solution.py:76
  134.3 8.9 %all-to-all-start.3 = ((bf16[4,256,4,128]{3,2,0,1:T(4,128)(2,1)}), bf16[4,256,4,128]{3,2,0,1:T(4,128)(2,1)}, u32[]{:S(2)}, u32[]{:S(2)}) async-start(bf16[4,256,4,128]{3,2,0,1:T(4,128)(2,1)} %copy.120), calls=%async_computation.3 | async-start | bytes 2097152 | tf_op jit(solution)/shard_map/all_to_all | solution.py:90
  145.9 3.0 collective-permute-start.1
  150.7 3.8 %collective-permute-start = (bf16[256,4,128]{2,0,1:T(8,128)(2,1)}, bf16[256,4,128]{2,0,1:T(8,128)(2,1)}, u32[]{:S(2)}, u32[]{:S(2)}) collective-permute-start(bf16[256,4,128]{2,0,1:T(8,128)(2,1)} %copy.101), channel_id=1, source_target_pairs={{0,4},{4,8},{8,12},{12,16},{16,20},{20,24},{24,28},{28,32},{32,36}... | collective-permute-start | bytes 786440 | tf_op jit(solution)/shard_map/ppermute | solution.py:13
  178.5 3.1 fusion.8
  181.6 21.9 %all-to-all-start.2 = ((bf16[256,4,4]{2,1,0:T(4,128)(2,1)}), bf16[256,4,4]{2,1,0:T(4,128)(2,1)S(1)}, u32[]{:S(2)}, u32[]{:S(2)}) async-start(bf16[256,4,4]{2,1,0:T(4,128)(2,1)} %copy.116), calls=%async_computation.2 | async-start | bytes 524288 | tf_op jit(solution)/shard_map/all_to_all | solution.py:123
  206.8 7.4 %all-to-all-done.2 = bf16[256,4,4]{2,1,0:T(4,128)(2,1)S(1)} async-done(((bf16[256,4,4]{2,1,0:T(4,128)(2,1)}), bf16[256,4,4]{2,1,0:T(4,128)(2,1)S(1)}, u32[]{:S(2)}, u32[]{:S(2)}) %all-to-all-start.2) | async-done | bytes 8224 | tf_op jit(solution)/shard_map/all_to_all | solution.py:123
  214.1 6.1 %all-to-all-start.5 = ((bf16[256,4,4]{2,1,0:T(4,128)(2,1)}), bf16[256,4,4]{2,1,0:T(4,128)(2,1)}, u32[]{:S(2)}, u32[]{:S(2)}) async-start(bf16[256,4,4]{2,1,0:T(4,128)(2,1)} %copy.128), calls=%async_computation.5 | async-start | bytes 524288 | tf_op jit(solution)/shard_map/all_to_all | solution.py:126
  220.2 4.2 %fusion.21 = bf16[256,4,4,128]{0,3,2,1:T(8,128)(2,1)} fusion(f32[256,4,4]{0,2,1:T(4,128)S(1)} %get-tuple-element.8, bf16[256,4,4,128]{3,0,2,1:T(8,128)(2,1)S(1)} %bitcast.115, f32[4,4,256,256]{2,3,1,0:T(8,128)} %get-tuple-element.13, f32[4,4,256]{2,1,0:T(4,128)S(1)} %get-tuple-element.12, pred[256,256]{0,1:T(8,128)(4,1)S(1)} %iota_compare_fusion.2), kind=kOutput, calls=%fused_computation.29 | convolution fusion | flops 273678336 | bytes 6389760 | tf_op jit(solution)/shard_map/chrs,schd->rchd/dot_general | solution.py:108
  227.2 3.5 %all-to-all-done.5 = bf16[256,4,4]{2,1,0:T(4,128)(2,1)} async-done(((bf16[256,4,4]{2,1,0:T(4,128)(2,1)}), bf16[256,4,4]{2,1,0:T(4,128)(2,1)}, u32[]{:S(2)}, u32[]{:S(2)}) %all-to-all-start.5) | async-done | bytes 8224 | tf_op jit(solution)/shard_map/all_to_all | solution.py:126
  230.7 7.3 %all-to-all-start.4 = ((bf16[256,4,4,128]{3,2,1,0:T(4,128)(2,1)}), bf16[256,4,4,128]{3,2,1,0:T(4,128)(2,1)}, u32[]{:S(2)}, u32[]{:S(2)}) async-start(bf16[256,4,4,128]{3,2,1,0:T(4,128)(2,1)} %copy.125), calls=%async_computation.4 | async-start | bytes 2097152 | tf_op jit(solution)/shard_map/all_to_all | solution.py:122
  238.3 3.5 %select_reduce_fusion = (f32[4,4,256]{2,1,0:T(4,128)S(1)}, f32[4,4,256,512]{3,2,1,0:T(8,128)S(1)}) fusion(pred[4,256,512]{2,1,0:T(8,128)(4,1)} %broadcast_and_fusion, bf16[4,256,4,128]{3,1,2,0:T(8,128)(2,1)} %copy.108, bf16[4,256,4,128]{3,2,1,0:T(4,128)(2,1)S(1)} %copy-done.3, bf16[4,256,4,128]{3,1,0,2:T(8,128)(2,1)} %bitcast.114), kind=kOutput, calls=%fused_computation.1 | convolution fusion | flops 547352576 | bytes 12075008 | tf_op jit(solution)/shard_map/bthd,buhd->bhtu/dot_general | solution.py:51
  241.8 3.2 copy-done.1
  245.1 3.8 %fusion.26 = f32[4,256,4,128]{1,3,2,0:T(8,128)} fusion(f32[4,4,256,512]{3,2,1,0:T(8,128)S(1)} %get-tuple-element.11, f32[4,4,256]{2,1,0:T(4,128)S(1)} %get-tuple-element.10, pred[4,256,512]{2,1,0:T(8,128)(4,1)S(1)} %copy-done.5, bf16[4,256,4,128]{1,3,2,0:T(8,128)(2,1)S(1)} %copy-done.9, bf16[4,256,4,128]{1,3,2,0:T(8,128)(2,1)S(1)} %copy-done.10), kind=kOutput, calls=%fused_computation.34 | convolution fusion | flops 549453824 | bytes 13123584 | tf_op jit(solution)/shard_map/bhtu,buhd->bthd/dot_general | solution.py:66
  251.9 5.0 %fusion = f32[4,4,256]{2,1,0:T(4,128)S(1)} fusion(f32[4,4,256,512]{3,2,1,0:T(8,128)} %copy-done.1, f32[4,4,256]{2,1,0:T(4,128)S(1)} %get-tuple-element.10, pred[4,256,512]{2,1,0:T(8,128)(4,1)S(1)} %copy-done.6), kind=kLoop, calls=%fused_computation.2 | loop fusion | flops 8384512 | bytes 8945664 | tf_op jit(solution)/shard_map/reduce_sum | solution.py:65
  272.2 4.6 %convolution_convert_fusion = bf16[1024,2048]{1,0:T(8,128)(2,1)} fusion(bf16[512,2048]{1,0:T(8,128)(2,1)S(1)} %copy-done, f32[128,8,4,128]{3,2,1,0:T(4,128)S(1)} %bitcast.109, f32[128,8,4,128]{3,2,1,0:T(4,128)S(1)} %bitcast.107, f32[128,8,4,128]{3,2,1,0:T(4,128)S(1)} %bitcast.111, f32[128,8,4,128]{3,2,1,0:T(4,128)S(1)} %bitcast.108, ...), kind=kOutput, calls=%fused_computation.11 | convolution fusion | flops 2152202240 | bytes 16777216 | tf_op jit(solution)/shard_map/dot_general | solution.py:143
  276.8 59.7 %reduce-scatter.2.cloned.1.call-done = bf16[256,2048]{1,0:T(8,128)(2,1)} async-done(((bf16[1024,2048]{1,0:T(8,128)(2,1)}), bf16[256,2048]{1,0:T(8,128)(2,1)}) %reduce-scatter.2.cloned.1.call-update) | async-done | bytes 1048592 | tf_op jit(solution)/shard_map/reduce_scatter | solution.py:142
  (83 shorter events, 68.0 us)
Async XLA Ops:
  6.5 265.7 %copy-start = (bf16[512,2048]{1,0:T(8,128)(2,1)S(1)}, bf16[512,2048]{1,0:T(8,128)(2,1)}, u32[]{:S(2)}) copy-start(bf16[512,2048]{1,0:T(8,128)(2,1)} %param.9) | copy-start | bytes 6291460
  6.5 47.9 %all-gather.2.cloned.1.call-start = ((), (), s32[]{:S(2)}) async-start(), calls=%async_computation.7 | async-start | bytes 5242880 | tf_op jit(solution)/shard_map/all_gather | solution.py:21
  64.8 37.0 %all-to-all-start.1 = ((bf16[4,256,4,128]{3,2,0,1:T(4,128)(2,1)}), bf16[4,256,4,128]{3,2,0,1:T(4,128)(2,1)}, u32[]{:S(2)}, u32[]{:S(2)}) async-start(bf16[4,256,4,128]{3,2,0,1:T(4,128)(2,1)} %copy.113), calls=%async_computation.1 | async-start | bytes 2097152 | tf_op jit(solution)/shard_map/all_to_all | solution.py:83
  101.8 32.5 %all-to-all-start = ((bf16[4,256,4,128]{3,2,0,1:T(4,128)(2,1)}), bf16[4,256,4,128]{3,2,0,1:T(4,128)(2,1)}, u32[]{:S(2)}, u32[]{:S(2)}) async-start(bf16[4,256,4,128]{3,2,0,1:T(4,128)(2,1)} %copy.111), calls=%async_computation | async-start | bytes 2097152 | tf_op jit(solution)/shard_map/all_to_all | solution.py:76
  121.2 23.9 %slice-start = ((bf16[1024,512]{0,1:T(8,128)(2,1)}), bf16[256,512]{0,1:T(8,128)(2,1)S(1)}, s32[]{:S(2)}) async-start(bf16[1024,512]{0,1:T(8,128)(2,1)} %convolution_convert_fusion.1), calls=%async_computation.9 | async-start | bytes 524288 | tf_op jit(solution)/shard_map/slice | solution.py:31
  134.3 47.3 %all-to-all-start.3 = ((bf16[4,256,4,128]{3,2,0,1:T(4,128)(2,1)}), bf16[4,256,4,128]{3,2,0,1:T(4,128)(2,1)}, u32[]{:S(2)}, u32[]{:S(2)}) async-start(bf16[4,256,4,128]{3,2,0,1:T(4,128)(2,1)} %copy.120), calls=%async_computation.3 | async-start | bytes 2097152 | tf_op jit(solution)/shard_map/all_to_all | solution.py:90
  145.9 23.9 %collective-permute-start.1 = (bf16[256,4,128]{2,0,1:T(8,128)(2,1)}, bf16[256,4,128]{2,0,1:T(8,128)(2,1)S(1)}, u32[]{:S(2)}, u32[]{:S(2)}) collective-permute-start(bf16[256,4,128]{2,0,1:T(8,128)(2,1)} %copy.105), channel_id=1, source_target_pairs={{0,4},{4,8},{8,12},{12,16},{16,20},{20,24},{24,28},{28,32},{32,36}... | collective-permute-start | bytes 786440 | tf_op jit(solution)/shard_map/ppermute | solution.py:13
  150.7 14.6 %collective-permute-start = (bf16[256,4,128]{2,0,1:T(8,128)(2,1)}, bf16[256,4,128]{2,0,1:T(8,128)(2,1)}, u32[]{:S(2)}, u32[]{:S(2)}) collective-permute-start(bf16[256,4,128]{2,0,1:T(8,128)(2,1)} %copy.101), channel_id=1, source_target_pairs={{0,4},{4,8},{8,12},{12,16},{16,20},{20,24},{24,28},{28,32},{32,36}... | collective-permute-start | bytes 786440 | tf_op jit(solution)/shard_map/ppermute | solution.py:13
  157.1 4.8 %copy-start.2 = (bf16[1024,512]{0,1:T(8,128)(2,1)S(1)}, bf16[1024,512]{0,1:T(8,128)(2,1)}, u32[]{:S(2)}) copy-start(bf16[1024,512]{0,1:T(8,128)(2,1)} %convolution_convert_fusion.1) | copy-start | bytes 3145732
  163.2 6.7 %copy-start.4 = (bf16[1024,4,128]{2,0,1:T(8,128)(2,1)S(1)}, bf16[1024,4,128]{2,0,1:T(8,128)(2,1)}, u32[]{:S(2)}) copy-start(bf16[1024,4,128]{2,0,1:T(8,128)(2,1)} %copy.106) | copy-start | bytes 3145732
  181.6 32.5 %all-to-all-start.2 = ((bf16[256,4,4]{2,1,0:T(4,128)(2,1)}), bf16[256,4,4]{2,1,0:T(4,128)(2,1)S(1)}, u32[]{:S(2)}, u32[]{:S(2)}) async-start(bf16[256,4,4]{2,1,0:T(4,128)(2,1)} %copy.116), calls=%async_computation.2 | async-start | bytes 524288 | tf_op jit(solution)/shard_map/all_to_all | solution.py:123
  214.1 16.6 %all-to-all-start.5 = ((bf16[256,4,4]{2,1,0:T(4,128)(2,1)}), bf16[256,4,4]{2,1,0:T(4,128)(2,1)}, u32[]{:S(2)}, u32[]{:S(2)}) async-start(bf16[256,4,4]{2,1,0:T(4,128)(2,1)} %copy.128), calls=%async_computation.5 | async-start | bytes 524288 | tf_op jit(solution)/shard_map/all_to_all | solution.py:126
  224.4 13.9 %copy-start.3 = (bf16[4,256,4,128]{3,2,1,0:T(4,128)(2,1)S(1)}, bf16[4,256,4,128]{3,2,1,0:T(4,128)(2,1)}, u32[]{:S(2)}) copy-start(bf16[4,256,4,128]{3,2,1,0:T(4,128)(2,1)} %reshape_reshape.13) | copy-start | bytes 3145732
  230.7 34.7 %all-to-all-start.4 = ((bf16[256,4,4,128]{3,2,1,0:T(4,128)(2,1)}), bf16[256,4,4,128]{3,2,1,0:T(4,128)(2,1)}, u32[]{:S(2)}, u32[]{:S(2)}) async-start(bf16[256,4,4,128]{3,2,1,0:T(4,128)(2,1)} %copy.125), calls=%async_computation.4 | async-start | bytes 2097152 | tf_op jit(solution)/shard_map/all_to_all | solution.py:122
  238.0 98.5 %reduce-scatter.2.cloned.1.call-start = ((), (), s32[]{:S(2)}) async-start(), calls=%async_computation.8 | async-start | bytes 5242880 | tf_op jit(solution)/shard_map/reduce_scatter | solution.py:142
  238.3 6.8 %copy-start.5 = (pred[4,256,512]{2,1,0:T(8,128)(4,1)S(1)}, pred[4,256,512]{2,1,0:T(8,128)(4,1)}, u32[]{:S(2)}) copy-start(pred[4,256,512]{2,1,0:T(8,128)(4,1)} %broadcast_and_fusion) | copy-start | bytes 1572868
  238.3 6.8 %copy-start.9 = (bf16[4,256,4,128]{1,3,2,0:T(8,128)(2,1)S(1)}, bf16[4,256,4,128]{1,3,2,0:T(8,128)(2,1)}, u32[]{:S(2)}) copy-start(bf16[4,256,4,128]{1,3,2,0:T(8,128)(2,1)} %copy.104) | copy-start | bytes 3145732
  238.3 6.8 %copy-start.10 = (bf16[4,256,4,128]{1,3,2,0:T(8,128)(2,1)S(1)}, bf16[4,256,4,128]{1,3,2,0:T(8,128)(2,1)}, u32[]{:S(2)}) copy-start(bf16[4,256,4,128]{1,3,2,0:T(8,128)(2,1)} %copy.103) | copy-start | bytes 3145732
  241.8 3.3 copy-start.1
  248.9 3.0 copy-start.6
  267.1 1.4 copy-start.7
  269.7 2.5 copy-start.8
Sparse Core Ops, SparseCore 0:
  9.2 45.2 all-gather.1
  277.0 59.5 reduce-scatter.1
where the time goes:
time: 345 us; the launch traced here: 343 us
  waiting for transfers between devices  149 us (43%)
  starting transfers between devices  69.4 us (20%)
  local copies, waits for them, and re-layouts  60.6 us (18%)
  matrix products  37.4 us (11%)
  between operations  13.7 us (4%)
  other arithmetic  12.9 us (4%)
    reduce_scatter x1, waiting for transfers between devices, shards(): lax.psum_scatter(jnp.dot(mixed, w_out, preferred_element_type=jnp.float32...  59.7 us
    all_gather x1, waiting for transfers between devices, shards(): shard_piece = lax.all_gather(tokens, 'head', axis=1, tiled=True)  47.2 us
    all_to_all x1, starting transfers between devices, shards(): lax.all_to_all(column_top.astype(jnp.bfloat16), 'seq', split_axis=0, conc...  21.9 us
    dot_general x3, matrix products, shards(): jnp.dot(shard_piece, weight, preferred_element_type=jnp.float32)  18.6 us
    all_to_all x1, waiting for transfers between devices, shards(): lax.all_to_all(key_heads.reshape(row_count, STRIDE, head_count, DH), 'seq...  15.6 us
    all_to_all x1, waiting for transfers between devices, shards(): lax.all_to_all(query.reshape(row_count, STRIDE, head_count, DH), 'seq', s...  13.1 us
    all_to_all x1, starting transfers between devices, shards(): lax.all_to_all(key_heads.reshape(row_count, STRIDE, head_count, DH), 'seq...  10.5 us
    all_to_all x1, starting transfers between devices, shards(): lax.all_to_all(value_heads.reshape(row_count, STRIDE, head_count, DH), 's...  8.9 us
  transfers between devices with their start and end apart: 10, of which 7 were waited for; matrix products, arithmetic and copies ran while one was open for 25% of the time, Pallas kernels for 0%

commit v1 on v0

v1 whole, which is shorter than its diff:
```python
import functools
import math

import jax
import jax.numpy as jnp
from jax import lax
from jax.experimental import pallas as pl
from jax.experimental.pallas import tpu as pltpu
from jax.sharding import PartitionSpec as P

MESH = pl.DeviceIdType.MESH
BF16 = jnp.bfloat16
F32 = jnp.float32
DH = 128
HEADS = 4
T = 1024
F = 512
BLK = 256
PIECE = 16
SEND = F + DH
SCALE2 = DH ** (-0.5) * math.log2(math.e)
NEG = -1e30


def dot(a, b):
    return jnp.dot(a, b, preferred_element_type=F32)


def dot_t(a, b):
    return lax.dot_general(a, b, (((1,), (1,)), ((), ())), preferred_element_type=F32)


def ds(start, size):
    return pl.ds(pl.multiple_of(start, size), size)


def iota(shape, dim):
    return lax.broadcasted_iota(jnp.int32, shape, dim)


def three_parts(value):
    parts = []
    for _ in range(3):
        part = value.astype(BF16).astype(F32)
        parts.append(part)
        value = value - part
    return parts


def kernel(
    tok, wq, wk, wv, wo, out,
    row_tok, class_tok, perm, arrived, w_in, w_o, row_acc, class_acc, qkv,
    col_f, col, ret, loc, loc_stat, send_mix, mix,
    load_sem, ag_s, ag_r, a2a_s, a2a_r, x_s, x_r, fwd_s, fwd_r, halo_s, halo_r,
    ret_s, ret_r, wo_s, wo_r, mix_s, mix_r,
):
    seq, h = lax.axis_index("seq"), lax.axis_index("head")
    n_seq = lax.axis_size("seq")
    hi, core = h // 2, h % 2
    z, x_lo, y = seq // 8, (seq // 4) % 2, seq % 4
    g = z * 4 + y
    groups = n_seq // 2
    half = (hi + x_lo) % 2
    other_seq = z * 8 + (1 - x_lo) * 4 + y
    sib = hi * 2 + 1 - core
    far = (1 - hi) * 2 + core

    def remote(src, dst, s_sem, r_sem, **device):
        return pltpu.make_async_remote_copy(
            src_ref=src, dst_ref=dst, send_sem=s_sem, recv_sem=r_sem,
            device_id=device, device_id_type=MESH,
        )

    def seq_of(group, x):
        return (group // 4) * 8 + x * 4 + group % 4

    barrier = pltpu.get_barrier_semaphore()

    def greet(k, carry):
        pl.semaphore_signal(
            barrier, inc=1, device_id={"seq": (seq + k) % n_seq}, device_id_type=MESH
        )
        return carry

    lax.fori_loop(1, n_seq, greet, 0)
    pl.semaphore_signal(barrier, inc=1, device_id={"head": sib}, device_id_type=MESH)
    for k in range(2):
        pl.semaphore_signal(
            barrier, inc=1, device_id={"head": (1 - hi) * 2 + k}, device_id_type=MESH
        )
    pl.semaphore_signal(
        barrier, inc=1, device_id={"seq": other_seq, "head": far}, device_id_type=MESH
    )

    own_lanes = ds(core * F, F)
    loads = [
        pltpu.make_async_copy(w, w_in.at[i], load_sem.at[i])
        for i, w in enumerate((wq, wk, wv))
    ]
    loads.append(pltpu.make_async_copy(wo, w_o.at[ds(h * F, F)], load_sem.at[3]))
    loads.append(pltpu.make_async_copy(tok, row_tok.at[hi, :, own_lanes], load_sem.at[4]))
    for load in loads:
        load.start()

    def permute(i, carry):
        j = iota((BLK, 1), 0)
        source = (
            ((j // 4) % 4) * BLK + ((i % 2) * 16 + j // 16) * 8 + (i // 2) * 4 + j % 4
        )
        pick = jnp.where(iota((BLK, T), 1) == source, 1.0, 0.0).astype(BF16)
        perm[i // 2, ds((i % 2) * BLK, BLK), :] = dot(pick, tok[...]).astype(BF16)
        return carry

    lax.fori_loop(0, 4, permute, 0)
    keep = pltpu.make_async_copy(
        perm.at[:, ds(g * PIECE, PIECE)], arrived.at[:, ds(g * PIECE, PIECE)], load_sem.at[5]
    )
    keep.start()

    pl.semaphore_wait(barrier, n_seq - 1 + 4)

    ag_far = remote(tok, row_tok.at[hi, :, own_lanes], ag_s.at[0], ag_r.at[0], head=far)
    ag_sib = remote(tok, row_tok.at[hi, :, own_lanes], ag_s.at[1], ag_r.at[1], head=sib)
    ag_far_block = row_tok.at[1 - hi, :, own_lanes]
    ag_fwd = remote(ag_far_block, ag_far_block, ag_s.at[2], ag_r.at[2], head=sib)

    def scatter(k, carry):
        to = (g + k) % groups
        remote(
            perm.at[:, ds(to * PIECE, PIECE)], arrived.at[:, ds(g * PIECE, PIECE)],
            a2a_s.at[0], a2a_r.at[0], seq=seq_of(to, x_lo),
        ).start()
        return carry

    lax.fori_loop(1, groups, scatter, 0)
    ag_far.start()
    ag_sib.start()

    def project(source, rows_of, write):
        def step(i, carry):
            n, b = i % 3, 3 - i // 3
            rows = ds(b * BLK, BLK)
            res = dot(source[rows, :], w_in[n, rows_of, :])
            for k in range(HEADS):
                write(n * HEADS + k, b, rows, res[:, k * DH : (k + 1) * DH])
            return carry

        return step

    def row_first(k, b, rows, res):
        row_acc[k, rows, :] = res

    def row_last(k, b, rows, res):
        qkv[k, ds((b + 1) * BLK, BLK), :] = (row_acc[k, rows, :] + res).astype(BF16)

    def class_first(k, b, rows, res):
        class_acc[k, rows, :] = res

    def class_last(k, b, rows, res):
        class_acc[k, rows, :] = class_acc[k, rows, :] + res

    own_rows, far_rows = ds(hi * 2 * F, 2 * F), ds((1 - hi) * 2 * F, 2 * F)
    for i in (0, 1, 2, 4):
        loads[i].wait()
    ag_sib.wait_recv()
    lax.fori_loop(0, 12, project(row_tok.at[hi], own_rows, row_first), 0)

    keep.wait()
    got = arrived.at[:, pl.ds(0, (groups - 1) * PIECE)]
    pltpu.make_async_copy(got, got, a2a_r.at[0]).wait()
    mine = lambda x: class_tok.at[hi, ds(x * F, F), own_lanes]
    theirs = lambda x: class_tok.at[1 - hi, ds(x * F, F), own_lanes]
    to_cross = remote(
        arrived.at[half], mine(x_lo), x_s.at[0], x_r.at[0], seq=other_seq, head=far
    )
    to_pair = remote(
        arrived.at[1 - half], mine(x_lo), x_s.at[1], x_r.at[1], seq=other_seq, head=h
    )
    to_far = remote(arrived.at[1 - half], mine(x_lo), x_s.at[2], x_r.at[2], seq=seq, head=far)
    to_sib = remote(arrived.at[half], mine(x_lo), x_s.at[3], x_r.at[3], seq=seq, head=sib)
    for copy in (to_far, to_cross, to_pair, to_sib):
        copy.start()
    stay = pltpu.make_async_copy(arrived.at[half], mine(x_lo), load_sem.at[6])
    stay.start()

    ag_far.wait_recv()
    ag_fwd.start()
    ag_fwd.wait_recv()
    lax.fori_loop(0, 12, project(row_tok.at[1 - hi], far_rows, row_last), 0)
    halo = remote(
        qkv.at[pl.ds(HEADS, 2 * HEADS), pl.ds(T, BLK)],
        qkv.at[pl.ds(HEADS, 2 * HEADS), pl.ds(0, BLK)],
        halo_s.at[0], halo_r.at[0], seq=(seq + 1) % n_seq,
    )
    halo.start()

    forwards = []
    for i, (copy, block) in enumerate(
        (
            (to_pair, mine(1 - x_lo)),
            (to_cross, theirs(1 - x_lo)),
            (to_far, theirs(x_lo)),
        )
    ):
        copy.wait_recv()
        forward = remote(block, block, fwd_s.at[i], fwd_r.at[i], head=sib)
        forward.start()
        forwards.append(forward)
    wo_mine = w_o.at[ds(h * F, F)]
    wo_theirs = w_o.at[ds(far * F, F)]
    wo_far = remote(wo, wo_mine, wo_s.at[0], wo_r.at[0], seq=other_seq, head=far)
    wo_sib = remote(wo, wo_mine, wo_s.at[1], wo_r.at[1], head=sib)
    wo_fwd = remote(wo_theirs, wo_theirs, wo_s.at[2], wo_r.at[2], head=sib)
    wo_far.start()
    wo_sib.start()

    to_sib.wait_recv()
    stay.wait()
    forwards[0].wait_recv()
    lax.fori_loop(0, 12, project(class_tok.at[hi], own_rows, class_first), 0)
    forwards[1].wait_recv()
    forwards[2].wait_recv()
    lax.fori_loop(0, 12, project(class_tok.at[1 - hi], far_rows, class_last), 0)

    def row_of(n):
        return ((n % 128) // 16) * 32 + (n // 128) * 16 + n % 16

    earlier = row_of(iota((BLK, BLK), 0)) > row_of(iota((BLK, BLK), 1))
    lane = iota((BLK, DH), 1)
    col_f[HEADS] = jnp.zeros((T, DH), F32)

    def column(k, carry):
        for c in range(4):
            at = pl.ds(c, BLK, stride=4)
            query = class_acc[k, at, :].astype(BF16)
            key = class_acc[HEADS + k, at, :].astype(BF16)
            value = class_acc[2 * HEADS + k, at, :].astype(BF16)
            scores = jnp.where(earlier, dot_t(query, key), NEG)
            top = jnp.max(scores, axis=1, keepdims=True)
            weights = jnp.where(earlier, jnp.exp2((scores - top) * SCALE2), 0.0)
            total = jnp.sum(weights, axis=1, keepdims=True)
            summed = dot(weights.astype(BF16), value)
            col_f[k, at, :] = summed * (1.0 / jnp.maximum(total, 1.0))
            stat = col_f[HEADS, at, :]
            for i, part in enumerate(three_parts(top * SCALE2) + three_parts(total)):
                stat = jnp.where(lane == k * 8 + i, part, stat)
            col_f[HEADS, at, :] = stat
        return carry

    lax.fori_loop(0, HEADS, column, 0)
    for k in range(HEADS + 1):
        col[:, k * DH : (k + 1) * DH] = col_f[k].astype(BF16)

    slot = ds((g * 2 + half) * PIECE, PIECE)

    def give_back(k, carry):
        to = (seq + k) % n_seq
        piece = ((to // 4) % 2) * F + ((to // 8) * 4 + to % 4) * PIECE
        remote(
            col.at[ds(piece, PIECE)], ret.at[slot], ret_s.at[0], ret_r.at[0], seq=to
        ).start()
        return carry

    lax.fori_loop(1, n_seq, give_back, 0)
    own_ret = pltpu.make_async_copy(
        col.at[ds(x_lo * F + g * PIECE, PIECE)], ret.at[slot], load_sem.at[7]
    )
    own_ret.start()

    halo.wait_recv()
    lower = iota((BLK, BLK), 1) <= iota((BLK, BLK), 0)

    def local(b, carry):
        before = jnp.where(jnp.logical_and(seq == 0, b == 0), NEG, 0.0)
        prev, cur = ds(b * BLK, BLK), ds((b + 1) * BLK, BLK)
        for k in range(HEADS):
            query = qkv[k, cur, :]
            s_cur = dot_t(query, qkv[HEADS + k, cur, :])
            s_prev = dot_t(query, qkv[HEADS + k, prev, :]) + before
            scores = jnp.where(lower, s_cur, s_prev)
            top = jnp.max(scores, axis=1, keepdims=True)
            weights = jnp.exp2((scores - top) * SCALE2)
            total = jnp.sum(weights, axis=1, keepdims=True)
            loc[k, prev, :] = dot(
                jnp.where(lower, weights, 0.0).astype(BF16), qkv[2 * HEADS + k, cur, :]
            ) + dot(
                jnp.where(lower, 0.0, weights).astype(BF16), qkv[2 * HEADS + k, prev, :]
            )
            loc_stat[k, prev, :] = top * SCALE2
            loc_stat[HEADS + k, prev, :] = total
        return carry

    lax.fori_loop(0, 4, local, 0)

    wo_far.wait_recv()
    wo_fwd.start()
    own_ret.wait()
    back = ret.at[pl.ds(0, (n_seq - 1) * PIECE)]
    pltpu.make_async_copy(back, back, ret_r.at[0]).wait()

    def merge(i, carry):
        b = ((hi + 1 - i // 2) % 2) * 2 + (core + (i + 1) // 2) % 2
        j = iota((BLK, 1), 0)
        source = (j // 4) * PIECE + b * 4 + j % 4
        pick = jnp.where(iota((BLK, T), 1) == source, 1.0, 0.0).astype(BF16)
        rows = ds(b * BLK, BLK)
        results = dot(pick, ret[...])
        for k in range(HEADS):
            at = F + k * 8
            part = [results[:, at + m : at + m + 1] for m in range(6)]
            col_top = part[0] + part[1] + part[2]
            col_total = part[3] + part[4] + part[5]
            top = jnp.maximum(loc_stat[k, rows, :], col_top)
            local_weight = jnp.exp2(loc_stat[k, rows, :] - top)
            col_weight = col_total * jnp.exp2(col_top - top)
            inv = 1.0 / (loc_stat[HEADS + k, rows, :] * local_weight + col_weight)
            send_mix[i, :, k * DH : (k + 1) * DH] = (
                loc[k, rows, :] * (local_weight * inv)
                + results[:, k * DH : (k + 1) * DH] * (col_weight * inv)
            ).astype(BF16)

        @pl.when(i < 3)
        def _():
            remote(
                send_mix.at[i], mix.at[hi, :, own_lanes], mix_s.at[i], mix_r.at[i], head=b
            ).start()

        return carry

    lax.fori_loop(0, 4, merge, 0)
    mix[hi, :, own_lanes] = send_mix[3]

    def mix_copy(i, b):
        return remote(
            send_mix.at[i], mix.at[hi, :, own_lanes], mix_s.at[i], mix_r.at[i], head=b
        )

    mix_copies = [mix_copy(0, far), mix_copy(1, (1 - hi) * 2 + 1 - core), mix_copy(2, sib)]
    loads[3].wait()
    wo_sib.wait_recv()
    mix_copies[2].wait_recv()
    outs = 4

    def out_first(i, carry):
        cols = ds(i * F, F)
        res = dot(mix[hi], w_o[own_rows, cols])
        for k in range(HEADS):
            row_acc[k, ds(i * BLK, BLK), :] = res[:, k * DH : (k + 1) * DH]
        return carry

    lax.fori_loop(0, outs, out_first, 0)
    wo_fwd.wait_recv()
    mix_copies[0].wait_recv()
    mix_copies[1].wait_recv()

    def out_last(i, carry):
        cols = ds(i * F, F)
        res = dot(mix[1 - hi], w_o[far_rows, cols])
        so_far = jnp.concatenate(
            [row_acc[k, ds(i * BLK, BLK), :] for k in range(HEADS)], axis=1
        )
        out[:, cols] = (res + so_far).astype(BF16)
        return carry

    lax.fori_loop(0, outs, out_last, 0)

    sent = perm.at[:, pl.ds(0, (groups - 1) * PIECE)]
    pltpu.make_async_copy(sent, sent, a2a_s.at[0]).wait()
    pltpu.make_async_copy(back, back, ret_s.at[0]).wait()
    for copy in (
        [ag_far, ag_sib, ag_fwd, to_cross, to_pair, to_far, to_sib, halo]
        + forwards + [wo_far, wo_sib, wo_fwd] + mix_copies
    ):
        copy.wait_send()


def shards(tokens, w_query, w_key, w_value, w_out):
    vmem = pl.BlockSpec(memory_space=pltpu.VMEM)
    anywhere = pl.BlockSpec(memory_space=pl.ANY)
    dma = lambda n: pltpu.SemaphoreType.DMA((n,))
    d = 4 * F
    return pl.pallas_call(
        kernel,
        out_shape=jax.ShapeDtypeStruct((BLK, d), BF16),
        in_specs=[vmem] + [anywhere] * 4,
        out_specs=vmem,
        scratch_shapes=[
            pltpu.VMEM((2, T, 2 * F), BF16),
            pltpu.VMEM((2, T, 2 * F), BF16),
            pltpu.VMEM((2, T // 2, F), BF16),
            pltpu.VMEM((2, T // 2, F), BF16),
            pltpu.VMEM((3, d, F), BF16),
            pltpu.VMEM((d, d), BF16),
            pltpu.VMEM((12, T, DH), F32),
            pltpu.VMEM((12, T, DH), F32),
            pltpu.VMEM((12, T + BLK, DH), BF16),
            pltpu.VMEM((HEADS + 1, T, DH), F32),
            pltpu.VMEM((T, SEND), BF16),
            pltpu.VMEM((T, SEND), BF16),
            pltpu.VMEM((HEADS, T, DH), F32),
            pltpu.VMEM((2 * HEADS, T, 1), F32),
            pltpu.VMEM((4, BLK, F), BF16),
            pltpu.VMEM((2, BLK, 2 * F), BF16),
            dma(8), dma(3), dma(3), dma(1), dma(1), dma(4), dma(4), dma(3), dma(3),
            dma(1), dma(1), dma(1), dma(1), dma(3), dma(3), dma(3), dma(3),
        ],
        compiler_params=pltpu.CompilerParams(
            collective_id=0, has_side_effects=True, vmem_limit_bytes=62 << 20
        ),
    )(tokens, w_query, w_key, w_value, w_out)


def solution(mesh):
    in_specs = (
        P("seq", "head"),
        P(None, "head"),
        P(None, "head"),
        P(None, "head"),
        P("head", None),
    )
    out_specs = P(("seq", "head"), None)
    return jax.shard_map(shards, mesh=mesh, in_specs=in_specs, out_specs=out_specs, check_vma=False)
```

time: 345 us -> 141 us (0.41)
  the two profiles are of different devices: /device:TPU:1 before, /device:TPU:2 now
where the time goes in v1:
time: 141 us
  Pallas kernels  139 us (99%)
  local copies, waits for them, and re-layouts  2.3 us (2%)
    pallas_call x1, Pallas kernels, shards(): pl.pallas_call(kernel, out_shape=jax.ShapeDtypeStruct((BLK, d), BF16), in...  139 us

profile of v1, /device:TPU:2, one launch (start us, length us, event | category | flops | bytes accessed | tf_op | source)
XLA Modules:
  0.0 140.8 jit_solution(9862068835582108163)
XLA Ops:
  0.0 138.5 %shard_map.55 = bf16[256,2048]{1,0:T(8,128)(2,1)} custom-call(bf16[1024,512]{1,0:T(8,128)(2,1)} %tok.1, bf16[2048,512]{1,0:T(8,128)(2,1)} %wq.1, bf16[2048,512]{1,0:T(8,128)(2,1)} %wk.1, bf16[2048,512]{1,0:T(8,128)(2,1)} %wv.1, bf16[512,2048]{1,0:T(8,128)(2,1)} %wo.1), custom_call_target="tpu_custom_call" | custom-call | tf_op jit(solution)/shard_map/pallas_call | solution.py:382
  138.5 2.3 %copy.7 = bf16[256,2048]{1,0:T(8,128)(2,1)} copy(bf16[256,2048]{1,0:T(8,128)(2,1)} %shard_map.55) | data formatting | bytes 2097152

commit v2 on v1

v2 whole, which is shorter than its diff:
```python
import functools
import math

import jax
import jax.numpy as jnp
from jax import lax
from jax.experimental import pallas as pl
from jax.experimental.pallas import tpu as pltpu
from jax.sharding import PartitionSpec as P

MESH = pl.DeviceIdType.MESH
BF16 = jnp.bfloat16
F32 = jnp.float32
DH = 128
HEADS = 4
T = 1024
F = 512
BLK = 256
PIECE = 16
LOG2E = math.log2(math.e)
SCALE2 = DH ** (-0.5) * LOG2E
NEG = -1e30


def dot(a, b):
    return jnp.dot(a, b, preferred_element_type=F32)


def dot_t(a, b):
    return lax.dot_general(a, b, (((1,), (1,)), ((), ())), preferred_element_type=F32)


def ds(start, size):
    return pl.ds(pl.multiple_of(start, size), size)


def iota(shape, dim):
    return lax.broadcasted_iota(jnp.int32, shape, dim)


def three_parts(value):
    parts = []
    for _ in range(3):
        part = value.astype(BF16)
        parts.append(part)
        value = value - part.astype(F32)
    return parts


def select_dot(pick, value):
    return sum(dot(pick, part) for part in three_parts(value))


def one_hot(hit):
    return jnp.where(hit, 1.0, 0.0).astype(BF16)


def kernel(
    tok, wq, wk, wv, wo, out,
    row_tok, class_tok, perm, arrived, w_in, w_o, row_acc, class_acc, qkv,
    col_f, col, ret, col_stat, ret_stat, loc, loc_stat, send_mix, mix,
    load_sem, ag_s, ag_r, a2a_s, a2a_r, x_s, x_r, fwd_s, fwd_r, halo_s, halo_r,
    ret_s, ret_r, stat_s, stat_r, wo_s, wo_r, mix_s, mix_r,
):
    seq, h = lax.axis_index("seq"), lax.axis_index("head")
    n_seq = lax.axis_size("seq")
    hi, core = h // 2, h % 2
    z, x_lo, y = seq // 8, (seq // 4) % 2, seq % 4
    g = z * 4 + y
    groups = n_seq // 2
    other_seq = z * 8 + (1 - x_lo) * 4 + y
    sib = hi * 2 + 1 - core
    far = (1 - hi) * 2 + core
    far_sib = (1 - hi) * 2 + 1 - core

    def remote(src, dst, s_sem, r_sem, **device):
        return pltpu.make_async_remote_copy(
            src_ref=src, dst_ref=dst, send_sem=s_sem, recv_sem=r_sem,
            device_id=device, device_id_type=MESH,
        )

    def seq_of(group, x):
        return (group // 4) * 8 + x * 4 + group % 4

    def wait_for(ref, sem):
        pltpu.make_async_copy(ref, ref, sem).wait()

    barrier = pltpu.get_barrier_semaphore()

    def greet(k, carry):
        pl.semaphore_signal(
            barrier, inc=1, device_id={"seq": (seq + k) % n_seq}, device_id_type=MESH
        )
        return carry

    lax.fori_loop(1, n_seq, greet, 0)
    for peer in (sib, far, far_sib):
        pl.semaphore_signal(barrier, inc=1, device_id={"head": peer}, device_id_type=MESH)
    pl.semaphore_signal(
        barrier, inc=1, device_id={"seq": other_seq, "head": far}, device_id_type=MESH
    )

    own_lanes = ds(core * F, F)
    own_rows, far_rows = ds(hi * 2 * F, 2 * F), ds((1 - hi) * 2 * F, 2 * F)
    loads = [
        pltpu.make_async_copy(w, w_in.at[i], load_sem.at[i])
        for i, w in enumerate((wq, wk, wv))
    ]
    loads.append(pltpu.make_async_copy(wo, w_o.at[ds(h * F, F)], load_sem.at[3]))
    loads.append(pltpu.make_async_copy(tok, row_tok.at[hi, :, own_lanes], load_sem.at[4]))
    for load in loads:
        load.start()

    def permute(i, carry):
        j = iota((BLK, 1), 0)
        source = (
            ((j // 4) % 4) * BLK + ((i % 2) * 16 + j // 16) * 8 + (i // 2) * 4 + j % 4
        )
        pick = one_hot(iota((BLK, T), 1) == source)
        perm[i // 2, ds((i % 2) * BLK, BLK), :] = dot(pick, tok[...]).astype(BF16)
        return carry

    lax.fori_loop(0, 4, permute, 0)
    here = ds(g * PIECE, PIECE)
    keeps = [
        pltpu.make_async_copy(perm.at[x, here], arrived.at[i, here], load_sem.at[5 + i])
        for i, x in enumerate((x_lo, 1 - x_lo))
    ]
    for keep in keeps:
        keep.start()

    pl.semaphore_wait(barrier, n_seq - 1 + 4)

    def scatter(i, x):
        def send(k, carry):
            to = (g + k) % groups
            remote(
                perm.at[x, ds(to * PIECE, PIECE)], arrived.at[i, here],
                a2a_s.at[i], a2a_r.at[i], seq=seq_of(to, x_lo),
            ).start()
            return carry

        lax.fori_loop(1, groups, send, 0)

    def rows_to_far(i):
        rows = pl.ds((1 - i) * 2 * BLK, 2 * BLK)
        theirs = row_tok.at[1 - hi, rows, own_lanes]
        return (
            remote(tok.at[rows], row_tok.at[hi, rows, own_lanes], ag_s.at[i], ag_r.at[i], head=far),
            remote(theirs, theirs, ag_s.at[2 + i], ag_r.at[2 + i], head=sib),
        )

    ag_far, ag_fwd = zip(rows_to_far(0), rows_to_far(1))
    ag_sib = remote(tok, row_tok.at[hi, :, own_lanes], ag_s.at[4], ag_r.at[4], head=sib)
    quarter = T // 8

    def wo_quarter(of, which):
        return w_o.at[ds(of * F + which * quarter, quarter)]

    wo_far = remote(
        wo.at[ds(y * quarter, quarter)], wo_quarter(h, y), wo_s.at[0], wo_r.at[0],
        seq=other_seq, head=far,
    )
    wo_sib = remote(wo, w_o.at[ds(h * F, F)], wo_s.at[1], wo_r.at[1], head=sib)
    wo_spread = [
        remote(
            wo_quarter(far, y), wo_quarter(far, y), wo_s.at[2 + k], wo_r.at[2 + k],
            seq=seq - y + (y + k) % 4,
        )
        for k in range(1, 4)
    ]
    wo_theirs = w_o.at[ds(far * F, F)]
    wo_fwd = remote(wo_theirs, wo_theirs, wo_s.at[2], wo_r.at[2], head=sib)

    scatter(0, x_lo)
    ag_far[0].start()
    ag_sib.start()
    scatter(1, 1 - x_lo)
    wo_far.start()
    wo_sib.start()

    def project(source, rows_of, first_row, blocks, write, heads=(0, HEADS)):
        lo, hi_ = heads

        def step(i, carry):
            n, b = i % 3, blocks - 1 - i // 3
            rows = ds(first_row + b * BLK, BLK)
            res = dot(source[rows, :], w_in[n, rows_of, lo * DH : hi_ * DH])
            for k in range(lo, hi_):
                write(n * HEADS + k, rows, res[:, (k - lo) * DH : (k - lo + 1) * DH])
            return carry

        lax.fori_loop(0, 3 * blocks, step, 0)

    def row_first(k, rows, res):
        row_acc[k, rows, :] = res

    def row_last(k, rows, res):
        behind = ds(rows.start + BLK, BLK)
        qkv[k, behind, :] = (row_acc[k, rows, :] + res).astype(BF16)

    def class_first(k, rows, res):
        class_acc[k, rows, :] = res

    def class_last(k, rows, res):
        class_acc[k, rows, :] = class_acc[k, rows, :] + res

    for i in (0, 1, 2, 4):
        loads[i].wait()
    ag_sib.wait_recv()
    project(row_tok.at[hi], own_rows, 0, 4, row_first)

    def mine(x):
        return class_tok.at[hi, ds(x * F, F), own_lanes]

    def theirs(x):
        return class_tok.at[1 - hi, ds(x * F, F), own_lanes]

    to_far = remote(arrived.at[0], mine(x_lo), x_s.at[0], x_r.at[0], head=far)
    to_sib = remote(arrived.at[0], mine(x_lo), x_s.at[1], x_r.at[1], head=sib)
    to_pair = remote(arrived.at[1], mine(x_lo), x_s.at[2], x_r.at[2], seq=other_seq)
    to_cross = remote(
        arrived.at[1], mine(x_lo), x_s.at[3], x_r.at[3], seq=other_seq, head=far
    )
    stay = pltpu.make_async_copy(arrived.at[0], mine(x_lo), load_sem.at[7])

    def forward(i, block):
        return remote(block, block, fwd_s.at[i], fwd_r.at[i], head=sib)

    fwd_far, fwd_pair, fwd_cross = (
        forward(0, theirs(x_lo)), forward(1, mine(1 - x_lo)), forward(2, theirs(1 - x_lo))
    )

    pieces = pl.ds(0, (groups - 1) * PIECE)
    keeps[0].wait()
    wait_for(arrived.at[0, pieces], a2a_r.at[0])
    to_far.start()
    to_sib.start()
    stay.start()

    ag_far[0].wait_recv()
    ag_fwd[0].start()
    wo_far.wait_recv()
    for copy in wo_spread:
        copy.start()
    ag_fwd[0].wait_recv()

    keeps[1].wait()
    wait_for(arrived.at[1, pieces], a2a_r.at[1])
    to_cross.start()
    to_pair.start()

    project(row_tok.at[1 - hi], far_rows, 2 * BLK, 2, row_last)
    halo = remote(
        qkv.at[pl.ds(HEADS, 2 * HEADS), pl.ds(T, BLK)],
        qkv.at[pl.ds(HEADS, 2 * HEADS), pl.ds(0, BLK)],
        halo_s.at[0], halo_r.at[0], seq=(seq + 1) % n_seq,
    )
    to_far.wait_recv()
    fwd_far.start()
    to_sib.wait_recv()
    stay.wait()
    project(class_tok.at[hi], own_rows, x_lo * F, 2, class_first)
    fwd_far.wait_recv()
    project(class_tok.at[1 - hi], far_rows, x_lo * F, 2, class_last)

    to_pair.wait_recv()
    fwd_pair.start()
    to_cross.wait_recv()
    fwd_cross.start()
    ag_far[1].start()
    halo.start()
    fwd_pair.wait_recv()
    project(class_tok.at[hi], own_rows, (1 - x_lo) * F, 2, class_first)
    fwd_cross.wait_recv()

    def row_of(n):
        return ((n % 128) // 16) * 32 + (n // 128) * 16 + n % 16

    earlier = row_of(iota((BLK, BLK), 0)) > row_of(iota((BLK, BLK), 1))
    lane = iota((BLK, DH), 1)
    place = (iota((BLK, DH), 0) % 4) * 32
    slot = g * 2 + x_lo
    own_ret = []
    for pair in range(2):
        heads = (2 * pair, 2 * pair + 2)
        project(class_tok.at[1 - hi], far_rows, (1 - x_lo) * F, 2, class_last, heads)

        def column(k, stat):
            for c in range(4):
                at = pl.ds(c, BLK, stride=4)
                head = 2 * pair + k
                query = class_acc[head, at, :].astype(BF16)
                key = class_acc[HEADS + head, at, :].astype(BF16)
                value = class_acc[2 * HEADS + head, at, :].astype(BF16)
                scores = jnp.where(earlier, dot_t(query, key), NEG)
                top = jnp.max(scores, axis=1, keepdims=True)
                weights = jnp.where(earlier, jnp.exp2((scores - top) * SCALE2), 0.0)
                total = jnp.maximum(jnp.sum(weights, axis=1, keepdims=True), 1.0)
                col_f[k, at, :] = dot(weights.astype(BF16), value) * (1.0 / total)
                level = top * SCALE2 + jnp.log(total) * LOG2E
                stat = jnp.where(lane == place + c * 8 + k, level, stat)
            return stat

        stat = lax.fori_loop(0, 2, column, jnp.zeros((BLK, DH), F32))
        for k in range(2):
            col[pair, :, k * DH : (k + 1) * DH] = col_f[k].astype(BF16)
        gather4 = one_hot(iota((n_seq, BLK), 1) // 4 == iota((n_seq, BLK), 0))
        col_stat[pair, :, 0, :] = select_dot(gather4, stat)

        def copies(to):
            at = ((to // 4) % 2) * groups + (to // 8) * 4 + to % 4
            return (
                (col.at[pair, ds(at * PIECE, PIECE)], ret.at[pair, ds(slot * PIECE, PIECE)]),
                (col_stat.at[pair, at], ret_stat.at[pair, slot]),
            )

        def give_back(k, carry):
            to = (seq + k) % n_seq
            values, stats = copies(to)
            remote(*stats, stat_s.at[pair], stat_r.at[pair], seq=to).start()
            remote(*values, ret_s.at[pair], ret_r.at[pair], seq=to).start()
            return carry

        lax.fori_loop(1, n_seq, give_back, 0)
        for i, (src, dst) in enumerate(copies(seq)):
            own_ret.append(pltpu.make_async_copy(src, dst, load_sem.at[8 + 2 * pair + i]))
            own_ret[-1].start()

    ag_far[1].wait_recv()
    ag_fwd[1].start()
    ag_fwd[1].wait_recv()
    project(row_tok.at[1 - hi], far_rows, 0, 2, row_last)
    for copy in wo_spread:
        copy.wait_recv()
    wo_fwd.start()
    halo.wait_recv()
    lower = iota((BLK, BLK), 1) <= iota((BLK, BLK), 0)

    def local(i, carry):
        b = 3 - i
        before = jnp.where(jnp.logical_and(seq == 0, b == 0), NEG, 0.0)
        prev, cur = ds(b * BLK, BLK), ds((b + 1) * BLK, BLK)
        for k in range(HEADS):
            query = qkv[k, cur, :]
            s_cur = dot_t(query, qkv[HEADS + k, cur, :])
            s_prev = dot_t(query, qkv[HEADS + k, prev, :]) + before
            scores = jnp.where(lower, s_cur, s_prev)
            top = jnp.max(scores, axis=1, keepdims=True)
            weights = jnp.exp2((scores - top) * SCALE2)
            total = jnp.sum(weights, axis=1, keepdims=True)
            loc[k, prev, :] = dot(
                jnp.where(lower, weights, 0.0).astype(BF16), qkv[2 * HEADS + k, cur, :]
            ) + dot(
                jnp.where(lower, 0.0, weights).astype(BF16), qkv[2 * HEADS + k, prev, :]
            )
            loc_stat[k, prev, :] = top * SCALE2
            loc_stat[HEADS + k, prev, :] = total
        return carry

    lax.fori_loop(0, 4, local, 0)

    def mix_copy(pair, i, b):
        lanes = pl.ds(pl.multiple_of(core * F + pair * 2 * DH, 2 * DH), 2 * DH)
        return remote(
            send_mix.at[pair, i], mix.at[hi, :, lanes],
            mix_s.at[pair, i], mix_r.at[pair, i], head=b,
        )

    for pair in range(2):
        own_ret[2 * pair].wait()
        own_ret[2 * pair + 1].wait()
        wait_for(ret_stat.at[pair, pl.ds(0, n_seq - 1)], stat_r.at[pair])
        wait_for(ret.at[pair, pl.ds(0, (n_seq - 1) * PIECE)], ret_r.at[pair])
        levels = three_parts(ret_stat[pair, :, 0, :])

        def merge(i, carry):
            b = ((hi + 1 - i // 2) % 2) * 2 + (core + (i + 1) // 2) % 2
            j = iota((BLK, 1), 0)
            pick = one_hot(iota((BLK, T), 1) == (j // 4) * PIECE + b * 4 + j % 4)
            rows = ds(b * BLK, BLK)
            results = dot(pick, ret[pair])
            pick = one_hot(iota((BLK, n_seq), 1) == j // 4)
            spread = sum(dot(pick, part) for part in levels)
            for k in range(2):
                head = 2 * pair + k
                level = jnp.sum(
                    jnp.where(lane == (b * 4 + j % 4) * 8 + k, spread, 0.0),
                    axis=1, keepdims=True,
                )
                top = jnp.maximum(loc_stat[head, rows, :], level)
                local_weight = jnp.exp2(loc_stat[head, rows, :] - top)
                col_weight = jnp.exp2(level - top)
                inv = 1.0 / (loc_stat[HEADS + head, rows, :] * local_weight + col_weight)
                send_mix[pair, i, :, k * DH : (k + 1) * DH] = (
                    loc[head, rows, :] * (local_weight * inv)
                    + results[:, k * DH : (k + 1) * DH] * (col_weight * inv)
                ).astype(BF16)

            @pl.when(i < 3)
            def _():
                mix_copy(pair, i, b).start()

            return carry

        lax.fori_loop(0, 4, merge, 0)
        mix[hi, :, pl.ds(pl.multiple_of(core * F + pair * 2 * DH, 2 * DH), 2 * DH)] = (
            send_mix[pair, 3]
        )

    mix_copies = [
        mix_copy(pair, i, b) for pair in range(2) for i, b in enumerate((far, far_sib, sib))
    ]
    loads[3].wait()
    wo_sib.wait_recv()
    mix_copies[2].wait_recv()
    mix_copies[5].wait_recv()

    def out_first(i, carry):
        res = dot(mix[hi], w_o[own_rows, ds(i * F, F)])
        for k in range(HEADS):
            row_acc[k, ds(i * BLK, BLK), :] = res[:, k * DH : (k + 1) * DH]
        return carry

    lax.fori_loop(0, 4, out_first, 0)
    wo_fwd.wait_recv()
    for i in (0, 1, 3, 4):
        mix_copies[i].wait_recv()

    def out_last(i, carry):
        res = dot(mix[1 - hi], w_o[far_rows, ds(i * F, F)])
        so_far = jnp.concatenate(
            [row_acc[k, ds(i * BLK, BLK), :] for k in range(HEADS)], axis=1
        )
        out[:, ds(i * F, F)] = (res + so_far).astype(BF16)
        return carry

    lax.fori_loop(0, 4, out_last, 0)

    for i in range(2):
        wait_for(perm.at[i, pieces], a2a_s.at[i])
        wait_for(col.at[i, pl.ds(0, (n_seq - 1) * PIECE)], ret_s.at[i])
        wait_for(col_stat.at[i, pl.ds(0, n_seq - 1)], stat_s.at[i])
    for copy in (
        *ag_far, *ag_fwd, ag_sib, to_far, to_sib, to_pair, to_cross,
        fwd_far, fwd_pair, fwd_cross, halo, wo_far, wo_sib, *wo_spread, wo_fwd, *mix_copies,
    ):
        copy.wait_send()


def shards(tokens, w_query, w_key, w_value, w_out):
    vmem = pl.BlockSpec(memory_space=pltpu.VMEM)
    anywhere = pl.BlockSpec(memory_space=pl.ANY)
    dma = lambda n: pltpu.SemaphoreType.DMA((n,))
    d = 4 * F
    n_seq = lax.axis_size("seq")
    return pl.pallas_call(
        kernel,
        out_shape=jax.ShapeDtypeStruct((BLK, d), BF16),
        in_specs=[vmem] + [anywhere] * 4,
        out_specs=vmem,
        scratch_shapes=[
            pltpu.VMEM((2, T, 2 * F), BF16),
            pltpu.VMEM((2, T, 2 * F), BF16),
            pltpu.VMEM((2, T // 2, F), BF16),
            pltpu.VMEM((2, T // 2, F), BF16),
            pltpu.VMEM((3, d, F), BF16),
            pltpu.VMEM((d, d), BF16),
            pltpu.VMEM((12, T, DH), F32),
            pltpu.VMEM((12, T, DH), F32),
            pltpu.VMEM((12, T + BLK, DH), BF16),
            pltpu.VMEM((2, T, DH), F32),
            pltpu.VMEM((2, T, 2 * DH), BF16),
            pltpu.VMEM((2, T, 2 * DH), BF16),
            pltpu.VMEM((2, n_seq, 1, DH), F32),
            pltpu.VMEM((2, n_seq, 1, DH), F32),
            pltpu.VMEM((HEADS, T, DH), F32),
            pltpu.VMEM((2 * HEADS, T, 1), F32),
            pltpu.VMEM((2, 4, BLK, 2 * DH), BF16),
            pltpu.VMEM((2, BLK, 2 * F), BF16),
            dma(12), dma(5), dma(5), dma(2), dma(2), dma(4), dma(4), dma(3), dma(3),
            dma(1), dma(1), dma(2), dma(2), dma(2), dma(2), dma(6), dma(6),
            pltpu.SemaphoreType.DMA((2, 3)), pltpu.SemaphoreType.DMA((2, 3)),
        ],
        compiler_params=pltpu.CompilerParams(
            collective_id=0, has_side_effects=True, vmem_limit_bytes=62 << 20
        ),
    )(tokens, w_query, w_key, w_value, w_out)


def solution(mesh):
    in_specs = (
        P("seq", "head"),
        P(None, "head"),
        P(None, "head"),
        P(None, "head"),
        P("head", None),
    )
    out_specs = P(("seq", "head"), None)
    return jax.shard_map(shards, mesh=mesh, in_specs=in_specs, out_specs=out_specs, check_vma=False)
```

time: 141 us -> 129 us (0.915)
  the two profiles are of different devices: /device:TPU:2 before, /device:TPU:1 now
where the time goes in v2:
time: 129 us; the launch traced here: 126 us
  Pallas kernels  124 us (96%)
  local copies, waits for them, and re-layouts  2.3 us (2%)
    pallas_call x1, Pallas kernels, shards(): pl.pallas_call(kernel, out_shape=jax.ShapeDtypeStruct((BLK, d), BF16), in...  124 us

profile of v2, /device:TPU:1, one launch (start us, length us, event | category | flops | bytes accessed | tf_op | source)
XLA Modules:
  0.0 126.4 jit_solution(9724897066860408541)
XLA Ops:
  0.0 124.0 %shard_map.55 = bf16[256,2048]{1,0:T(8,128)(2,1)} custom-call(bf16[1024,512]{1,0:T(8,128)(2,1)} %tok.1, bf16[2048,512]{1,0:T(8,128)(2,1)} %wq.1, bf16[2048,512]{1,0:T(8,128)(2,1)} %wk.1, bf16[2048,512]{1,0:T(8,128)(2,1)} %wv.1, bf16[512,2048]{1,0:T(8,128)(2,1)} %wo.1), custom_call_target="tpu_custom_call" | custom-call | tf_op jit(solution)/shard_map/pallas_call | solution.py:457
  124.1 2.3 %copy.7 = bf16[256,2048]{1,0:T(8,128)(2,1)} copy(bf16[256,2048]{1,0:T(8,128)(2,1)} %shard_map.55) | data formatting | bytes 2097152

commit v3 on v2

--- a/solution.py
+++ b/solution.py
@@ -153,30 +153,39 @@
     ag_far, ag_fwd = zip(rows_to_far(0), rows_to_far(1))
     ag_sib = remote(tok, row_tok.at[hi, :, own_lanes], ag_s.at[4], ag_r.at[4], head=sib)
     quarter = T // 8
-
-    def wo_quarter(of, which):
-        return w_o.at[ds(of * F + which * quarter, quarter)]
-
+    eighth = quarter // 2
+
+    def wo_quarter(which):
+        return w_o.at[ds(far * F + which * quarter, quarter)]
+
+    at = y * quarter + x_lo * eighth
     wo_far = remote(
-        wo.at[ds(y * quarter, quarter)], wo_quarter(h, y), wo_s.at[0], wo_r.at[0],
+        wo.at[ds(at, eighth)], w_o.at[ds(h * F + at, eighth)], wo_s.at[0], wo_r.at[0],
         seq=other_seq, head=far,
     )
     wo_sib = remote(wo, w_o.at[ds(h * F, F)], wo_s.at[1], wo_r.at[1], head=sib)
+    got = w_o.at[ds(far * F + y * quarter + (1 - x_lo) * eighth, eighth)]
+    wo_pair = remote(got, got, wo_s.at[2], wo_r.at[2], seq=other_seq)
     wo_spread = [
         remote(
-            wo_quarter(far, y), wo_quarter(far, y), wo_s.at[2 + k], wo_r.at[2 + k],
+            wo_quarter(y), wo_quarter(y), wo_s.at[2 + k], wo_r.at[2 + k],
             seq=seq - y + (y + k) % 4,
         )
         for k in range(1, 4)
     ]
-    wo_theirs = w_o.at[ds(far * F, F)]
-    wo_fwd = remote(wo_theirs, wo_theirs, wo_s.at[2], wo_r.at[2], head=sib)
-
+    wo_fwd = [
+        remote(
+            wo_quarter((y - k + 4) % 4), wo_quarter((y - k + 4) % 4),
+            wo_s.at[6 + k], wo_r.at[6 + k], head=sib,
+        )
+        for k in range(4)
+    ]
+
+    wo_far.start()
     scatter(0, x_lo)
     ag_far[0].start()
     ag_sib.start()
     scatter(1, 1 - x_lo)
-    wo_far.start()
     wo_sib.start()
 
     def project(source, rows_of, first_row, blocks, write, heads=(0, HEADS)):
@@ -238,24 +247,27 @@
     to_sib.start()
     stay.start()
 
+    wo_far.wait_recv()
+    wo_pair.start()
     ag_far[0].wait_recv()
     ag_fwd[0].start()
-    wo_far.wait_recv()
-    for copy in wo_spread:
-        copy.start()
     ag_fwd[0].wait_recv()
-
-    keeps[1].wait()
-    wait_for(arrived.at[1, pieces], a2a_r.at[1])
-    to_cross.start()
-    to_pair.start()
-
     project(row_tok.at[1 - hi], far_rows, 2 * BLK, 2, row_last)
     halo = remote(
         qkv.at[pl.ds(HEADS, 2 * HEADS), pl.ds(T, BLK)],
         qkv.at[pl.ds(HEADS, 2 * HEADS), pl.ds(0, BLK)],
         halo_s.at[0], halo_r.at[0], seq=(seq + 1) % n_seq,
     )
+    keeps[1].wait()
+    wait_for(arrived.at[1, pieces], a2a_r.at[1])
+    to_cross.start()
+    to_pair.start()
+    halo.start()
+    wo_pair.wait_recv()
+    for copy in wo_spread:
+        copy.start()
+    wo_fwd[0].start()
+
     to_far.wait_recv()
     fwd_far.start()
     to_sib.wait_recv()
@@ -264,77 +276,6 @@
     fwd_far.wait_recv()
     project(class_tok.at[1 - hi], far_rows, x_lo * F, 2, class_last)
 
-    to_pair.wait_recv()
-    fwd_pair.start()
-    to_cross.wait_recv()
-    fwd_cross.start()
-    ag_far[1].start()
-    halo.start()
-    fwd_pair.wait_recv()
-    project(class_tok.at[hi], own_rows, (1 - x_lo) * F, 2, class_first)
-    fwd_cross.wait_recv()
-
-    def row_of(n):
-        return ((n % 128) // 16) * 32 + (n // 128) * 16 + n % 16
-
-    earlier = row_of(iota((BLK, BLK), 0)) > row_of(iota((BLK, BLK), 1))
-    lane = iota((BLK, DH), 1)
-    place = (iota((BLK, DH), 0) % 4) * 32
-    slot = g * 2 + x_lo
-    own_ret = []
-    for pair in range(2):
-        heads = (2 * pair, 2 * pair + 2)
-        project(class_tok.at[1 - hi], far_rows, (1 - x_lo) * F, 2, class_last, heads)
-
-        def column(k, stat):
-            for c in range(4):
-                at = pl.ds(c, BLK, stride=4)
-                head = 2 * pair + k
-                query = class_acc[head, at, :].astype(BF16)
-                key = class_acc[HEADS + head, at, :].astype(BF16)
-                value = class_acc[2 * HEADS + head, at, :].astype(BF16)
-                scores = jnp.where(earlier, dot_t(query, key), NEG)
-                top = jnp.max(scores, axis=1, keepdims=True)
-                weights = jnp.where(earlier, jnp.exp2((scores - top) * SCALE2), 0.0)
-                total = jnp.maximum(jnp.sum(weights, axis=1, keepdims=True), 1.0)
-                col_f[k, at, :] = dot(weights.astype(BF16), value) * (1.0 / total)
-                level = top * SCALE2 + jnp.log(total) * LOG2E
-                stat = jnp.where(lane == place + c * 8 + k, level, stat)
-            return stat
-
-        stat = lax.fori_loop(0, 2, column, jnp.zeros((BLK, DH), F32))
-        for k in range(2):
-            col[pair, :, k * DH : (k + 1) * DH] = col_f[k].astype(BF16)
-        gather4 = one_hot(iota((n_seq, BLK), 1) // 4 == iota((n_seq, BLK), 0))
-        col_stat[pair, :, 0, :] = select_dot(gather4, stat)
-
-        def copies(to):
-            at = ((to // 4) % 2) * groups + (to // 8) * 4 + to % 4
-            return (
-                (col.at[pair, ds(at * PIECE, PIECE)], ret.at[pair, ds(slot * PIECE, PIECE)]),
-                (col_stat.at[pair, at], ret_stat.at[pair, slot]),
-            )
-
-        def give_back(k, carry):
-            to = (seq + k) % n_seq
-            values, stats = copies(to)
-            remote(*stats, stat_s.at[pair], stat_r.at[pair], seq=to).start()
-            remote(*values, ret_s.at[pair], ret_r.at[pair], seq=to).start()
-            return carry
-
-        lax.fori_loop(1, n_seq, give_back, 0)
-        for i, (src, dst) in enumerate(copies(seq)):
-            own_ret.append(pltpu.make_async_copy(src, dst, load_sem.at[8 + 2 * pair + i]))
-            own_ret[-1].start()
-
-    ag_far[1].wait_recv()
-    ag_fwd[1].start()
-    ag_fwd[1].wait_recv()
-    project(row_tok.at[1 - hi], far_rows, 0, 2, row_last)
-    for copy in wo_spread:
-        copy.wait_recv()
-    wo_fwd.start()
-    halo.wait_recv()
     lower = iota((BLK, BLK), 1) <= iota((BLK, BLK), 0)
 
     def local(i, carry):
@@ -358,7 +299,79 @@
             loc_stat[HEADS + k, prev, :] = total
         return carry
 
-    lax.fori_loop(0, 4, local, 0)
+    lax.fori_loop(0, 1, local, 0)
+
+    to_pair.wait_recv()
+    fwd_pair.start()
+    to_cross.wait_recv()
+    fwd_cross.start()
+    ag_far[1].start()
+    fwd_pair.wait_recv()
+    project(class_tok.at[hi], own_rows, (1 - x_lo) * F, 2, class_first)
+    fwd_cross.wait_recv()
+
+    def row_of(n):
+        return ((n % 128) // 16) * 32 + (n // 128) * 16 + n % 16
+
+    earlier = row_of(iota((BLK, BLK), 0)) > row_of(iota((BLK, BLK), 1))
+    lane = iota((BLK, DH), 1)
+    place = (iota((BLK, DH), 0) % 4) * 32
+    slot = g * 2 + x_lo
+    own_ret = []
+    for pair in range(2):
+        heads = (2 * pair, 2 * pair + 2)
+        project(class_tok.at[1 - hi], far_rows, (1 - x_lo) * F, 2, class_last, heads)
+
+        def column(k, stat):
+            for c in range(4):
+                at = pl.ds(c, BLK, stride=4)
+                head = 2 * pair + k
+                query = class_acc[head, at, :].astype(BF16)
+                key = class_acc[HEADS + head, at, :].astype(BF16)
+                value = class_acc[2 * HEADS + head, at, :].astype(BF16)
+                scores = jnp.where(earlier, dot_t(query, key), NEG)
+                top = jnp.max(scores, axis=1, keepdims=True)
+                weights = jnp.where(earlier, jnp.exp2((scores - top) * SCALE2), 0.0)
+                total = jnp.maximum(jnp.sum(weights, axis=1, keepdims=True), 1.0)
+                col_f[k, at, :] = dot(weights.astype(BF16), value) * (1.0 / total)
+                level = top * SCALE2 + jnp.log(total) * LOG2E
+                stat = jnp.where(lane == place + c * 8 + k, level, stat)
+            return stat
+
+        stat = lax.fori_loop(0, 2, column, jnp.zeros((BLK, DH), F32))
+        for k in range(2):
+            col[pair, :, k * DH : (k + 1) * DH] = col_f[k].astype(BF16)
+        gather4 = one_hot(iota((n_seq, BLK), 1) // 4 == iota((n_seq, BLK), 0))
+        col_stat[pair, :, 0, :] = select_dot(gather4, stat)
+
+        def copies(to):
+            at = ((to // 4) % 2) * groups + (to // 8) * 4 + to % 4
+            return (
+                (col.at[pair, ds(at * PIECE, PIECE)], ret.at[pair, ds(slot * PIECE, PIECE)]),
+                (col_stat.at[pair, at], ret_stat.at[pair, slot]),
+            )
+
+        def give_back(k, carry):
+            to = (seq + k) % n_seq
+            values, stats = copies(to)
+            remote(*stats, stat_s.at[pair], stat_r.at[pair], seq=to).start()
+            remote(*values, ret_s.at[pair], ret_r.at[pair], seq=to).start()
+            return carry
+
+        lax.fori_loop(1, n_seq, give_back, 0)
+        for i, (src, dst) in enumerate(copies(seq)):
+            own_ret.append(pltpu.make_async_copy(src, dst, load_sem.at[8 + 2 * pair + i]))
+            own_ret[-1].start()
+
+    ag_far[1].wait_recv()
+    ag_fwd[1].start()
+    ag_fwd[1].wait_recv()
+    project(row_tok.at[1 - hi], far_rows, 0, 2, row_last)
+    for k in range(3):
+        wo_spread[k].wait_recv()
+        wo_fwd[k + 1].start()
+    halo.wait_recv()
+    lax.fori_loop(1, 4, local, 0)
 
     def mix_copy(pair, i, b):
         lanes = pl.ds(pl.multiple_of(core * F + pair * 2 * DH, 2 * DH), 2 * DH)
@@ -423,7 +436,8 @@
         return carry
 
     lax.fori_loop(0, 4, out_first, 0)
-    wo_fwd.wait_recv()
+    for copy in wo_fwd:
+        copy.wait_recv()
     for i in (0, 1, 3, 4):
         mix_copies[i].wait_recv()
 
@@ -443,7 +457,8 @@
         wait_for(col_stat.at[i, pl.ds(0, n_seq - 1)], stat_s.at[i])
     for copy in (
         *ag_far, *ag_fwd, ag_sib, to_far, to_sib, to_pair, to_cross,
-        fwd_far, fwd_pair, fwd_cross, halo, wo_far, wo_sib, *wo_spread, wo_fwd, *mix_copies,
+        fwd_far, fwd_pair, fwd_cross, halo, wo_far, wo_sib, wo_pair, *wo_spread, *wo_fwd,
+        *mix_copies,
     ):
         copy.wait_send()
 
@@ -479,7 +494,7 @@
             pltpu.VMEM((2, 4, BLK, 2 * DH), BF16),
             pltpu.VMEM((2, BLK, 2 * F), BF16),
             dma(12), dma(5), dma(5), dma(2), dma(2), dma(4), dma(4), dma(3), dma(3),
-            dma(1), dma(1), dma(2), dma(2), dma(2), dma(2), dma(6), dma(6),
+            dma(1), dma(1), dma(2), dma(2), dma(2), dma(2), dma(10), dma(10),
             pltpu.SemaphoreType.DMA((2, 3)), pltpu.SemaphoreType.DMA((2, 3)),
         ],
         compiler_params=pltpu.CompilerParams(

time: 129 us -> 124 us (0.961); the launches traced: 126 us -> 124 us
  Pallas kernels: 124 us -> 122 us
    pallas_call x1, Pallas kernels: 124 us -> 122 us  [shards(): pl.pallas_call(kernel, out_shape=jax.ShapeDtypeStruct((BLK, d), BF16), in...]
where the time goes in v3:
time: 124 us
  Pallas kernels  122 us (98%)
  local copies, waits for them, and re-layouts  2.3 us (2%)
    pallas_call x1, Pallas kernels, shards(): pl.pallas_call(kernel, out_shape=jax.ShapeDtypeStruct((BLK, d), BF16), in...  122 us

profile of v3, /device:TPU:1, one launch (start us, length us, event | category | flops | bytes accessed | tf_op | source)
XLA Modules:
  0.0 124.3 jit_solution(221123142828133267)
XLA Ops:
  0.0 122.0 %shard_map.55 = bf16[256,2048]{1,0:T(8,128)(2,1)} custom-call(bf16[1024,512]{1,0:T(8,128)(2,1)} %tok.1, bf16[2048,512]{1,0:T(8,128)(2,1)} %wq.1, bf16[2048,512]{1,0:T(8,128)(2,1)} %wk.1, bf16[2048,512]{1,0:T(8,128)(2,1)} %wv.1, bf16[512,2048]{1,0:T(8,128)(2,1)} %wo.1), custom_call_target="tpu_custom_call" | custom-call | tf_op jit(solution)/shard_map/pallas_call | solution.py:472
  122.0 2.3 %copy.7 = bf16[256,2048]{1,0:T(8,128)(2,1)} copy(bf16[256,2048]{1,0:T(8,128)(2,1)} %shard_map.55) | data formatting | bytes 2097152

commit v4 on v3

--- a/solution.py
+++ b/solution.py
@@ -143,29 +143,26 @@
         lax.fori_loop(1, groups, send, 0)
 
     def rows_to_far(i):
-        rows = pl.ds((1 - i) * 2 * BLK, 2 * BLK)
+        rows = pl.ds(*((3 * BLK, BLK), (2 * BLK, BLK), (0, 2 * BLK))[i])
         theirs = row_tok.at[1 - hi, rows, own_lanes]
         return (
             remote(tok.at[rows], row_tok.at[hi, rows, own_lanes], ag_s.at[i], ag_r.at[i], head=far),
-            remote(theirs, theirs, ag_s.at[2 + i], ag_r.at[2 + i], head=sib),
-        )
-
-    ag_far, ag_fwd = zip(rows_to_far(0), rows_to_far(1))
-    ag_sib = remote(tok, row_tok.at[hi, :, own_lanes], ag_s.at[4], ag_r.at[4], head=sib)
+            remote(theirs, theirs, ag_s.at[3 + i], ag_r.at[3 + i], head=sib),
+        )
+
+    ag_far, ag_fwd = zip(*(rows_to_far(i) for i in range(3)))
+    ag_sib = remote(tok, row_tok.at[hi, :, own_lanes], ag_s.at[6], ag_r.at[6], head=sib)
     quarter = T // 8
-    eighth = quarter // 2
 
     def wo_quarter(which):
         return w_o.at[ds(far * F + which * quarter, quarter)]
 
-    at = y * quarter + x_lo * eighth
+    at = y * quarter
     wo_far = remote(
-        wo.at[ds(at, eighth)], w_o.at[ds(h * F + at, eighth)], wo_s.at[0], wo_r.at[0],
+        wo.at[ds(at, quarter)], w_o.at[ds(h * F + at, quarter)], wo_s.at[0], wo_r.at[0],
         seq=other_seq, head=far,
     )
     wo_sib = remote(wo, w_o.at[ds(h * F, F)], wo_s.at[1], wo_r.at[1], head=sib)
-    got = w_o.at[ds(far * F + y * quarter + (1 - x_lo) * eighth, eighth)]
-    wo_pair = remote(got, got, wo_s.at[2], wo_r.at[2], seq=other_seq)
     wo_spread = [
         remote(
             wo_quarter(y), wo_quarter(y), wo_s.at[2 + k], wo_r.at[2 + k],
@@ -181,10 +178,11 @@
         for k in range(4)
     ]
 
+    ag_far[0].start()
+    scatter(0, x_lo)
+    ag_sib.start()
+    ag_far[1].start()
     wo_far.start()
-    scatter(0, x_lo)
-    ag_far[0].start()
-    ag_sib.start()
     scatter(1, 1 - x_lo)
     wo_sib.start()
 
@@ -217,7 +215,18 @@
     for i in (0, 1, 2, 4):
         loads[i].wait()
     ag_sib.wait_recv()
-    project(row_tok.at[hi], own_rows, 0, 4, row_first)
+    project(row_tok.at[hi], own_rows, 3 * BLK, 1, row_first)
+    ag_far[0].wait_recv()
+    ag_fwd[0].start()
+    ag_fwd[0].wait_recv()
+    project(row_tok.at[1 - hi], far_rows, 3 * BLK, 1, row_last)
+    halo = remote(
+        qkv.at[pl.ds(HEADS, 2 * HEADS), pl.ds(T, BLK)],
+        qkv.at[pl.ds(HEADS, 2 * HEADS), pl.ds(0, BLK)],
+        halo_s.at[0], halo_r.at[0], seq=(seq + 1) % n_seq,
+    )
+    halo.start()
+    project(row_tok.at[hi], own_rows, 0, 3, row_first)
 
     def mine(x):
         return class_tok.at[hi, ds(x * F, F), own_lanes]
@@ -247,23 +256,15 @@
     to_sib.start()
     stay.start()
 
-    wo_far.wait_recv()
-    wo_pair.start()
-    ag_far[0].wait_recv()
-    ag_fwd[0].start()
-    ag_fwd[0].wait_recv()
-    project(row_tok.at[1 - hi], far_rows, 2 * BLK, 2, row_last)
-    halo = remote(
-        qkv.at[pl.ds(HEADS, 2 * HEADS), pl.ds(T, BLK)],
-        qkv.at[pl.ds(HEADS, 2 * HEADS), pl.ds(0, BLK)],
-        halo_s.at[0], halo_r.at[0], seq=(seq + 1) % n_seq,
-    )
+    ag_far[1].wait_recv()
+    ag_fwd[1].start()
+    ag_fwd[1].wait_recv()
+    project(row_tok.at[1 - hi], far_rows, 2 * BLK, 1, row_last)
     keeps[1].wait()
     wait_for(arrived.at[1, pieces], a2a_r.at[1])
     to_cross.start()
     to_pair.start()
-    halo.start()
-    wo_pair.wait_recv()
+    wo_far.wait_recv()
     for copy in wo_spread:
         copy.start()
     wo_fwd[0].start()
@@ -305,7 +306,7 @@
     fwd_pair.start()
     to_cross.wait_recv()
     fwd_cross.start()
-    ag_far[1].start()
+    ag_far[2].start()
     fwd_pair.wait_recv()
     project(class_tok.at[hi], own_rows, (1 - x_lo) * F, 2, class_first)
     fwd_cross.wait_recv()
@@ -363,9 +364,9 @@
             own_ret.append(pltpu.make_async_copy(src, dst, load_sem.at[8 + 2 * pair + i]))
             own_ret[-1].start()
 
-    ag_far[1].wait_recv()
-    ag_fwd[1].start()
-    ag_fwd[1].wait_recv()
+    ag_far[2].wait_recv()
+    ag_fwd[2].start()
+    ag_fwd[2].wait_recv()
     project(row_tok.at[1 - hi], far_rows, 0, 2, row_last)
     for k in range(3):
         wo_spread[k].wait_recv()
@@ -457,7 +458,7 @@
         wait_for(col_stat.at[i, pl.ds(0, n_seq - 1)], stat_s.at[i])
     for copy in (
         *ag_far, *ag_fwd, ag_sib, to_far, to_sib, to_pair, to_cross,
-        fwd_far, fwd_pair, fwd_cross, halo, wo_far, wo_sib, wo_pair, *wo_spread, *wo_fwd,
+        fwd_far, fwd_pair, fwd_cross, halo, wo_far, wo_sib, *wo_spread, *wo_fwd,
         *mix_copies,
     ):
         copy.wait_send()
@@ -493,7 +494,7 @@
             pltpu.VMEM((2 * HEADS, T, 1), F32),
             pltpu.VMEM((2, 4, BLK, 2 * DH), BF16),
             pltpu.VMEM((2, BLK, 2 * F), BF16),
-            dma(12), dma(5), dma(5), dma(2), dma(2), dma(4), dma(4), dma(3), dma(3),
+            dma(12), dma(7), dma(7), dma(2), dma(2), dma(4), dma(4), dma(3), dma(3),
             dma(1), dma(1), dma(2), dma(2), dma(2), dma(2), dma(10), dma(10),
             pltpu.SemaphoreType.DMA((2, 3)), pltpu.SemaphoreType.DMA((2, 3)),
         ],

time: 124 us -> 114 us (0.919)
  Pallas kernels: 122 us -> 111 us
    pallas_call x1, Pallas kernels: 122 us -> 111 us  [shards(): pl.pallas_call(kernel, out_shape=jax.ShapeDtypeStruct((BLK, d), BF16), in...]
where the time goes in v4:
time: 114 us
  Pallas kernels  111 us (97%)
  local copies, waits for them, and re-layouts  2.3 us (2%)
    pallas_call x1, Pallas kernels, shards(): pl.pallas_call(kernel, out_shape=jax.ShapeDtypeStruct((BLK, d), BF16), in...  111 us
    unnamed x1, local copies, waits for them, and re-layouts  2.3 us

profile of v4, /device:TPU:1, one launch (start us, length us, event | category | flops | bytes accessed | tf_op | source)
XLA Modules:
  0.0 113.7 jit_solution(3449819361922356991)
XLA Ops:
  0.0 111.4 %shard_map.55 = bf16[256,2048]{1,0:T(8,128)(2,1)} custom-call(bf16[1024,512]{1,0:T(8,128)(2,1)} %tok.1, bf16[2048,512]{1,0:T(8,128)(2,1)} %wq.1, bf16[2048,512]{1,0:T(8,128)(2,1)} %wk.1, bf16[2048,512]{1,0:T(8,128)(2,1)} %wv.1, bf16[512,2048]{1,0:T(8,128)(2,1)} %wo.1), custom_call_target="tpu_custom_call" | custom-call | tf_op jit(solution)/shard_map/pallas_call | solution.py:473
  111.4 2.3 %copy.7 = bf16[256,2048]{1,0:T(8,128)(2,1)} copy(bf16[256,2048]{1,0:T(8,128)(2,1)} %shard_map.55) | data formatting | bytes 2097152

commit v5 on v4

--- a/solution.py
+++ b/solution.py
@@ -236,18 +236,34 @@
 
     to_far = remote(arrived.at[0], mine(x_lo), x_s.at[0], x_r.at[0], head=far)
     to_sib = remote(arrived.at[0], mine(x_lo), x_s.at[1], x_r.at[1], head=sib)
-    to_pair = remote(arrived.at[1], mine(x_lo), x_s.at[2], x_r.at[2], seq=other_seq)
-    to_cross = remote(
-        arrived.at[1], mine(x_lo), x_s.at[3], x_r.at[3], seq=other_seq, head=far
-    )
+    def part(i):
+        return pl.ds(i * BLK, BLK)
+
+    def place(c, x, i):
+        return class_tok.at[c, ds(x * F + i * BLK, BLK), own_lanes]
+
+    to_pair = [
+        remote(
+            arrived.at[1, part(i)], place(hi, x_lo, i), x_s.at[2 + i], x_r.at[2 + i],
+            seq=other_seq,
+        )
+        for i in range(2)
+    ]
+    to_cross = [
+        remote(
+            arrived.at[1, part(i)], place(hi, x_lo, i), x_s.at[4 + i], x_r.at[4 + i],
+            seq=other_seq, head=far,
+        )
+        for i in range(2)
+    ]
     stay = pltpu.make_async_copy(arrived.at[0], mine(x_lo), load_sem.at[7])
 
     def forward(i, block):
         return remote(block, block, fwd_s.at[i], fwd_r.at[i], head=sib)
 
-    fwd_far, fwd_pair, fwd_cross = (
-        forward(0, theirs(x_lo)), forward(1, mine(1 - x_lo)), forward(2, theirs(1 - x_lo))
-    )
+    fwd_far = forward(0, theirs(x_lo))
+    fwd_pair = [forward(1 + i, place(hi, 1 - x_lo, i)) for i in range(2)]
+    fwd_cross = [forward(3 + i, place(1 - hi, 1 - x_lo, i)) for i in range(2)]
 
     pieces = pl.ds(0, (groups - 1) * PIECE)
     keeps[0].wait()
@@ -262,8 +278,9 @@
     project(row_tok.at[1 - hi], far_rows, 2 * BLK, 1, row_last)
     keeps[1].wait()
     wait_for(arrived.at[1, pieces], a2a_r.at[1])
-    to_cross.start()
-    to_pair.start()
+    for i in range(2):
+        to_cross[i].start()
+        to_pair[i].start()
     wo_far.wait_recv()
     for copy in wo_spread:
         copy.start()
@@ -302,14 +319,23 @@
 
     lax.fori_loop(0, 1, local, 0)
 
-    to_pair.wait_recv()
-    fwd_pair.start()
-    to_cross.wait_recv()
-    fwd_cross.start()
+    def from_x(i):
+        to_pair[i].wait_recv()
+        fwd_pair[i].start()
+        to_cross[i].wait_recv()
+        fwd_cross[i].start()
+
+    def from_sib(i):
+        fwd_pair[i].wait_recv()
+        project(class_tok.at[hi], own_rows, (1 - x_lo) * F + i * BLK, 1, class_first)
+        fwd_cross[i].wait_recv()
+
+    from_x(0)
+    from_sib(0)
+    project(class_tok.at[1 - hi], far_rows, (1 - x_lo) * F, 1, class_last)
+    from_x(1)
     ag_far[2].start()
-    fwd_pair.wait_recv()
-    project(class_tok.at[hi], own_rows, (1 - x_lo) * F, 2, class_first)
-    fwd_cross.wait_recv()
+    from_sib(1)
 
     def row_of(n):
         return ((n % 128) // 16) * 32 + (n // 128) * 16 + n % 16
@@ -321,7 +347,7 @@
     own_ret = []
     for pair in range(2):
         heads = (2 * pair, 2 * pair + 2)
-        project(class_tok.at[1 - hi], far_rows, (1 - x_lo) * F, 2, class_last, heads)
+        project(class_tok.at[1 - hi], far_rows, (1 - x_lo) * F + BLK, 1, class_last, heads)
 
         def column(k, stat):
             for c in range(4):
@@ -457,8 +483,8 @@
         wait_for(col.at[i, pl.ds(0, (n_seq - 1) * PIECE)], ret_s.at[i])
         wait_for(col_stat.at[i, pl.ds(0, n_seq - 1)], stat_s.at[i])
     for copy in (
-        *ag_far, *ag_fwd, ag_sib, to_far, to_sib, to_pair, to_cross,
-        fwd_far, fwd_pair, fwd_cross, halo, wo_far, wo_sib, *wo_spread, *wo_fwd,
+        *ag_far, *ag_fwd, ag_sib, to_far, to_sib, *to_pair, *to_cross,
+        fwd_far, *fwd_pair, *fwd_cross, halo, wo_far, wo_sib, *wo_spread, *wo_fwd,
         *mix_copies,
     ):
         copy.wait_send()
@@ -494,7 +520,7 @@
             pltpu.VMEM((2 * HEADS, T, 1), F32),
             pltpu.VMEM((2, 4, BLK, 2 * DH), BF16),
             pltpu.VMEM((2, BLK, 2 * F), BF16),
-            dma(12), dma(7), dma(7), dma(2), dma(2), dma(4), dma(4), dma(3), dma(3),
+            dma(12), dma(7), dma(7), dma(2), dma(2), dma(6), dma(6), dma(5), dma(5),
             dma(1), dma(1), dma(2), dma(2), dma(2), dma(2), dma(10), dma(10),
             pltpu.SemaphoreType.DMA((2, 3)), pltpu.SemaphoreType.DMA((2, 3)),
         ],

time: 114 us -> 113 us (level)
  no operation moved by 1% of the time
where the time goes in v5:
time: 113 us
  Pallas kernels  111 us (98%)
  local copies, waits for them, and re-layouts  2.3 us (2%)
    pallas_call x1, Pallas kernels, shards(): pl.pallas_call(kernel, out_shape=jax.ShapeDtypeStruct((BLK, d), BF16), in...  111 us
    unnamed x1, local copies, waits for them, and re-layouts  2.3 us

profile of v5, /device:TPU:1, one launch (start us, length us, event | category | flops | bytes accessed | tf_op | source)
XLA Modules:
  0.0 112.9 jit_solution(13866409597928418788)
XLA Ops:
  0.0 110.6 %shard_map.55 = bf16[256,2048]{1,0:T(8,128)(2,1)} custom-call(bf16[1024,512]{1,0:T(8,128)(2,1)} %tok.1, bf16[2048,512]{1,0:T(8,128)(2,1)} %wq.1, bf16[2048,512]{1,0:T(8,128)(2,1)} %wk.1, bf16[2048,512]{1,0:T(8,128)(2,1)} %wv.1, bf16[512,2048]{1,0:T(8,128)(2,1)} %wo.1), custom_call_target="tpu_custom_call" | custom-call | tf_op jit(solution)/shard_map/pallas_call | solution.py:499
  110.6 2.3 %copy.7 = bf16[256,2048]{1,0:T(8,128)(2,1)} copy(bf16[256,2048]{1,0:T(8,128)(2,1)} %shard_map.55) | data formatting | bytes 2097152

commit v6 on v5

--- a/solution.py
+++ b/solution.py
@@ -182,7 +182,6 @@
     scatter(0, x_lo)
     ag_sib.start()
     ag_far[1].start()
-    wo_far.start()
     scatter(1, 1 - x_lo)
     wo_sib.start()
 
@@ -226,6 +225,7 @@
         halo_s.at[0], halo_r.at[0], seq=(seq + 1) % n_seq,
     )
     halo.start()
+    wo_far.start()
     project(row_tok.at[hi], own_rows, 0, 3, row_first)
 
     def mine(x):

time: 113 us -> 113 us (level)
  no operation moved by 1% of the time
where the time goes in v6:
time: 113 us
  Pallas kernels  111 us (98%)
  local copies, waits for them, and re-layouts  2.3 us (2%)
    pallas_call x1, Pallas kernels, shards(): pl.pallas_call(kernel, out_shape=jax.ShapeDtypeStruct((BLK, d), BF16), in...  111 us
    unnamed x1, local copies, waits for them, and re-layouts  2.3 us

profile of v6, /device:TPU:1, one launch (start us, length us, event | category | flops | bytes accessed | tf_op | source)
XLA Modules:
  0.0 112.9 jit_solution(2875729715656413175)
XLA Ops:
  0.0 110.6 %shard_map.55 = bf16[256,2048]{1,0:T(8,128)(2,1)} custom-call(bf16[1024,512]{1,0:T(8,128)(2,1)} %tok.1, bf16[2048,512]{1,0:T(8,128)(2,1)} %wq.1, bf16[2048,512]{1,0:T(8,128)(2,1)} %wk.1, bf16[2048,512]{1,0:T(8,128)(2,1)} %wv.1, bf16[512,2048]{1,0:T(8,128)(2,1)} %wo.1), custom_call_target="tpu_custom_call" | custom-call | tf_op jit(solution)/shard_map/pallas_call | solution.py:499
  110.6 2.3 %copy.7 = bf16[256,2048]{1,0:T(8,128)(2,1)} copy(bf16[256,2048]{1,0:T(8,128)(2,1)} %shard_map.55) | data formatting | bytes 2097152
